TPU v7x, 256 devices: a whole 4x4x8 slice. The times are simulated.
256 devices in a mesh: dp: 4 (over x), ctx: 64 (over z, y, core).
Axes of the slice: x: 4, y: 4, z: 8, core: 2. Of those that a mesh axis runs over, the one named last changes fastest.
Arguments:
- queries: bfloat16 [2, 32768, 2048], P(None, ('dp', 'ctx')), may hold values from -6 to 6
- keys: bfloat16 [2, 32768, 1024], P(None, ('dp', 'ctx')), may hold values from -6 to 6
- values: bfloat16 [2, 32768, 1024], P(None, ('dp', 'ctx')), may hold values from -6 to 6
- doc_start: int32 [2, 32768], P(None, ('dp', 'ctx')), may hold values from 0 to 16383, as said below
- gain_q: float32 [128], replicated, may hold values from 0.5 to 1.5
- key_norm_gain: float32 [128], replicated, may hold values from 0.5 to 1.5
- cotangent: bfloat16 [2, 32768, 2048], P(None, ('dp', 'ctx')), may hold values from -6 to 6
Outputs:
- attended: bfloat16 [2, 32768, 2048], P(None, ('dp', 'ctx'))
- grad_queries: bfloat16 [2, 32768, 2048], P(None, ('dp', 'ctx'))
- grad_keys: bfloat16 [2, 32768, 1024], P(None, ('dp', 'ctx'))
- value_gradients: bfloat16 [2, 32768, 1024], P(None, ('dp', 'ctx'))
- grad_gain_q: float32 [128], replicated
- grad_gain_k: float32 [128], replicated
Inputs may be any that keep to these rules, and one draw needn't show every extreme that they name: doc_start gives each token the position in its sequence of its document's first token; the documents of a sequence are runs of 1 to 256 tokens, the first starting at 0, and every sequence has one of exactly 256 tokens.
All inputs are finite; a program needn't handle non-finite values.
Results may differ from a plain program's by a relative error of at most 0.012.
Values may be sent and summed in bfloat16 or wider, within the bound.
No kernel may reach another device: no remote copies, remote signals or barrier semaphores. Data moves between devices by JAX's collectives and lax.ppermute only.
A program may use at most 128 MiB of HBM per device.

v0:
```python
from functools import partial

import jax
import jax.numpy as jnp
from jax import lax
from jax.sharding import PartitionSpec as P

REACH = 2


query_factor = 168.0 ** (-0.5)
rotary_base = 1000000.0
norm_epsilon = 1e-06


def from_behind(block, axis, distance):
    devices = range(lax.axis_size(axis))
    route = [(i - distance, i) for i in devices if i - distance in devices]
    return lax.ppermute(block, axis, route)


def rotary_angles(position, head_width):
    exponent = jnp.arange(head_width // 2, dtype=jnp.float32) * (2.0 / head_width)
    frequency = jnp.exp(-exponent * jnp.log(jnp.float32(rotary_base)))
    return position.astype(jnp.float32)[..., None] * frequency


def prepare(tensor, gain, angle, factor):
    inverse = lax.rsqrt(jnp.mean(tensor * tensor, axis=-1, keepdims=True) + norm_epsilon)
    normed = tensor * inverse * gain
    middle = tensor.shape[-1] // 2
    cosine = jnp.cos(angle)[..., None, :]
    sine = jnp.sin(angle)[..., None, :]
    first = normed[..., :middle]
    second = normed[..., middle:]
    return (
        jnp.concatenate([first * cosine - second * sine, second * cosine + first * sine], axis=-1)
        * factor
    )


def slot_positions(slot, rows, group, block):
    ascending = slot * block + rows
    descending = slot * block + block - 1 - rows
    inside = (slot >= 0) & (slot < 2 * group)
    return jnp.where(inside, jnp.where(slot < group, ascending, descending), -1)


def visible(doc_query, query_position, key_position):
    return (doc_query[:, :, None] <= key_position[:, None, :]) & (
        key_position[:, None, :] <= query_position[:, :, None]
    )


def forward_terms(q_rot, key_panel, value_panel, mask):
    scores = jnp.einsum("xihrd,xjhd->xhrij", q_rot, key_panel, preferred_element_type=jnp.float32)
    weights = jnp.where(mask[:, None, None], jnp.exp(scores), 0.0)
    summed = jnp.sum(weights, axis=-1)
    mixed = jnp.einsum(
        "xhrij,xjhd->xihrd",
        weights.astype(jnp.bfloat16),
        value_panel,
        preferred_element_type=jnp.float32,
    )
    return (summed, mixed)


def softmax_grads(q_rot, cotangent_heads, key_panel, value_panel, mask, total, delta):
    scores = jnp.einsum("xihrd,xjhd->xhrij", q_rot, key_panel, preferred_element_type=jnp.float32)
    probs = jnp.where(mask[:, None, None], jnp.exp(scores) / total[..., None], 0.0)
    dprob = jnp.einsum(
        "xihrd,xjhd->xhrij", cotangent_heads, value_panel, preferred_element_type=jnp.float32
    )
    dscore = probs * (dprob - delta[..., None])
    return (probs.astype(jnp.bfloat16), dscore.astype(jnp.bfloat16))


def key_grads(probs, dscore, q_rot, cotangent_heads):
    grad_key = jnp.einsum("xhrij,xihrd->xjhd", dscore, q_rot, preferred_element_type=jnp.float32)
    grad_value = jnp.einsum(
        "xhrij,xihrd->xjhd", probs, cotangent_heads, preferred_element_type=jnp.float32
    )
    return (grad_key, grad_value)


def all_grads(q_rot, cotangent_heads, key_panel, value_panel, mask, total, delta):
    probs, dscore = softmax_grads(
        q_rot, cotangent_heads, key_panel, value_panel, mask, total, delta
    )
    grad_key, grad_value = key_grads(probs, dscore, q_rot, cotangent_heads)
    grad_query = jnp.einsum(
        "xhrij,xjhd->xihrd", dscore, key_panel, preferred_element_type=jnp.float32
    )
    return (grad_query, grad_key, grad_value)


def advance(lower, upper, at_fold):
    moved_lower = from_behind(lower, "ctx", 1)
    moved_upper = from_behind(upper, "ctx", -1)
    return (moved_lower, jnp.where(at_fold, lower, moved_upper))


def retreat_grads(lower, upper, at_fold, at_start):
    moved_lower = from_behind(lower, "ctx", -1)
    moved_upper = from_behind(upper, "ctx", 1)
    return (jnp.where(at_fold, upper, moved_lower), jnp.where(at_start, 0.0, moved_upper))


def shards(queries, keys, values, doc_start, gain_q, key_norm_gain, cotangent):
    group = lax.axis_size("ctx")
    block = queries.shape[1]
    head_width = gain_q.shape[0]
    q_heads = queries.shape[2] // head_width
    kv_heads = keys.shape[2] // head_width
    repeat = q_heads // kv_heads
    group_index = lax.axis_index("ctx")
    at_fold = group_index == group - 1
    at_start = group_index == 0
    rows = jnp.arange(block, dtype=jnp.int32)[None, :]
    own_slot = jnp.stack([group_index, 2 * group - 1 - group_index])[:, None]
    own_position = slot_positions(own_slot, rows, group, block)
    angle = rotary_angles(own_position, head_width)
    q_rotated, q_back = jax.vjp(
        lambda tensor, gain: prepare(tensor, gain, angle, query_factor),
        queries.astype(jnp.float32).reshape(2, block, q_heads, head_width),
        gain_q,
    )
    q_rot = q_rotated.astype(jnp.bfloat16).reshape(2, block, kv_heads, repeat, head_width)
    k_rotated, k_back = jax.vjp(
        lambda tensor, gain: prepare(tensor, gain, angle, 1.0),
        keys.astype(jnp.float32).reshape(2, block, kv_heads, head_width),
        key_norm_gain,
    )
    k_rot = k_rotated.astype(jnp.bfloat16)
    cotangent_heads = cotangent.reshape(2, block, kv_heads, repeat, head_width)
    local_key_panel = jnp.stack([k_rot.reshape(2, block, -1), values], axis=1)
    panels = [local_key_panel]
    lower, upper = (local_key_panel[0], local_key_panel[1])
    for step in range(REACH):
        lower, upper = advance(lower, upper, at_fold)
        panels.append(jnp.stack([lower, upper]))
    masks = [
        visible(doc_start, own_position, slot_positions(own_slot - step, rows, group, block))
        for step in range(REACH + 1)
    ]
    zeros_q = jnp.zeros((2, block, kv_heads, repeat, head_width), jnp.float32)
    summed = jnp.zeros((2, kv_heads, repeat, block), jnp.float32)
    mixed = zeros_q
    key_panels = []
    value_panels = []
    for step in range(REACH + 1):
        key_panel = panels[step][:, 0].reshape(2, block, kv_heads, head_width)
        value_panel = panels[step][:, 1].reshape(2, block, kv_heads, head_width)
        key_panels.append(key_panel)
        value_panels.append(value_panel)
        compute = partial(forward_terms, q_rot, key_panel, value_panel, masks[step])
        if step == 0:
            terms = compute()
        else:
            terms = compute()
        summed = summed + terms[0]
        mixed = mixed + terms[1]
    attended_heads = (mixed / jnp.transpose(summed, (0, 3, 1, 2))[..., None]).astype(jnp.bfloat16)
    delta = jnp.einsum(
        "xihrd,xihrd->xhri", cotangent_heads, attended_heads, preferred_element_type=jnp.float32
    )
    grad_q_heads = zeros_q
    for step in range(REACH, -1, -1):
        compute = partial(
            all_grads,
            q_rot,
            cotangent_heads,
            key_panels[step],
            value_panels[step],
            masks[step],
            summed,
            delta,
        )
        if step == 0:
            terms = compute()
        else:
            terms = compute()
        grad_q_heads = grad_q_heads + terms[0]
        contribution = jnp.stack(
            [terms[1].reshape(2, block, -1), terms[2].reshape(2, block, -1)], axis=1
        )
        if step == REACH:
            carried_lower, carried_upper = (contribution[0], contribution[1])
        else:
            carried_lower, carried_upper = retreat_grads(
                carried_lower, carried_upper, at_fold, at_start
            )
            carried_lower = carried_lower + contribution[0]
            carried_upper = carried_upper + contribution[1]
    key_value_gradient = jnp.stack([carried_lower, carried_upper])
    grad_k_heads = key_value_gradient[:, 0].reshape(2, block, kv_heads, head_width)
    grad_v_flat = key_value_gradient[:, 1]
    grad_queries, grad_gain_q = q_back(grad_q_heads.reshape(2, block, q_heads, head_width))
    grad_keys, grad_gain_k = k_back(grad_k_heads)
    grad_gain_q, grad_gain_k = lax.psum((grad_gain_q, grad_gain_k), ("dp", "ctx"))
    return (
        attended_heads.reshape(2, block, -1),
        grad_queries.reshape(2, block, -1).astype(jnp.bfloat16),
        grad_keys.reshape(2, block, -1).astype(jnp.bfloat16),
        grad_v_flat.astype(jnp.bfloat16),
        grad_gain_q,
        grad_gain_k,
    )


def solution(mesh):
    placed = (
        P(None, ("dp", "ctx"), None),
        P(None, ("dp", "ctx"), None),
        P(None, ("dp", "ctx"), None),
        P(None, ("dp", "ctx")),
        P(),
        P(),
        P(None, ("dp", "ctx"), None),
    )
    return jax.shard_map(
        shards,
        mesh=mesh,
        in_specs=placed,
        out_specs=(
            P(None, ("dp", "ctx"), None),
            P(None, ("dp", "ctx"), None),
            P(None, ("dp", "ctx"), None),
            P(None, ("dp", "ctx"), None),
            P(),
            P(),
        ),
        check_vma=False,
    )
```

profile of v0, /device:TPU:1, one launch (start us, length us, event | category | flops | bytes accessed | tf_op | source)
XLA Modules:
  0.0 234.9 jit_solution(2773730723189249938)
XLA Ops:
  8.4 5.1 %collective-permute-start.1 = (bf16[2,128,1024]{1,2,0:T(8,128)(2,1)}, bf16[2,128,1024]{1,2,0:T(8,128)(2,1)}, u32[]{:S(2)}, u32[]{:S(2)}) collective-permute-start(bf16[2,128,1024]{1,2,0:T(8,128)(2,1)} %fusion.65), channel_id=1, source_target_pairs={{1,0},{2,1},{3,2},{4,3},{5,4},{6,5},{7,6},{8,7},{9,8},{10,9},{11,1... | collective-permute-start | bytes 1572872 | tf_op jit(solution)/shard_map/ppermute | solution.py:19
  17.4 2.0 copy.219
  19.3 1.9 copy.220
  21.5 2.9 %fusion.3 = bf16[2,128,8,2,128]{4,1,3,2,0:T(8,128)(2,1)S(1)} fusion(f32[2,128,8,2,64]{4,1,3,2,0:T(8,128)} %bitcast.308, f32[2,128,8,2,64]{4,1,3,2,0:T(8,128)} %bitcast.307), kind=kLoop, calls=%fused_computation.9 | loop fusion | flops 1572864 | bytes 3145728 | tf_op jit(solution)/shard_map/convert_element_type | solution.py:128
  25.4 2.1 broadcast_select_fusion
  27.5 1.9 collective-permute-start
  29.4 2.4 %fusion.15 = (f32[2,8,2,128]{3,2,1,0:T(2,128)}, f32[2,8,128,128,2]{3,2,4,1,0:T(8,128)}) fusion(pred[2,128,128]{1,2,0:T(8,128)(4,1)S(1)} %get-tuple-element.68, bf16[2,128,8,2,128]{4,1,3,2,0:T(8,128)(2,1)S(1)} %fusion.3, bf16[2,128,8,128]{3,1,2,0:T(8,128)(2,1)S(1)} %copy-done.9), kind=kOutput, calls=%fused_computation.48 | convolution fusion | flops 135262208 | bytes 3719168 | tf_op jit(solution)/shard_map/xihrd,xjhd->xhrij/dot_general | solution.py:56
  31.8 3.2 %collective-permute-start.3 = (bf16[2,128,1024]{1,2,0:T(8,128)(2,1)}, bf16[2,128,1024]{1,2,0:T(8,128)(2,1)}, u32[]{:S(2)}, u32[]{:S(2)}) collective-permute-start(bf16[2,128,1024]{1,2,0:T(8,128)(2,1)} %get-tuple-element.48), channel_id=1, source_target_pairs={{1,0},{2,1},{3,2},{4,3},{5,4},{6,5},{7,6},{8,7},{9,8},{10,9},{11,1... | collective-permute-start | bytes 1572872 | tf_op jit(solution)/shard_map/ppermute | solution.py:19
  35.9 2.6 %reshape.655 = bf16[2,128,8,2,128]{4,3,2,1,0:T(2,128)(2,1)} reshape(bf16[2,128,2048]{2,1,0:T(8,128)(2,1)} %param.13) | data formatting | bytes 2097152 | tf_op jit(solution)/shard_map/reshape | solution.py:135
  38.4 3.7 %copy.247 = bf16[2,128,8,2,128]{1,4,3,2,0:T(8,128)(2,1)} copy(bf16[2,128,8,2,128]{4,3,2,1,0:T(2,128)(2,1)} %reshape.655) | data formatting | bytes 2097152 | tf_op jit(solution)/shard_map/reshape | solution.py:135
  42.1 2.7 %collective-permute-start.2 = (bf16[2,128,1024]{1,2,0:T(8,128)(2,1)}, bf16[2,128,1024]{1,2,0:T(8,128)(2,1)S(1)}, u32[]{:S(2)}, u32[]{:S(2)}) collective-permute-start(bf16[2,128,1024]{1,2,0:T(8,128)(2,1)} %collective-permute-done), channel_id=1, source_target_pairs={{0,1},{1,2},{2,3},{3,4},{4,5},{5,6},{6,7},{7,8},{8,9},{9,10},{10,1... | collective-permute-start | bytes 1572872 | tf_op jit(solution)/shard_map/ppermute | solution.py:19
  48.7 2.3 collective-permute-done.2
  54.2 2.4 %bitcast_convert_fusion = (f32[2,8,2,128,128]{3,4,2,1,0:T(8,128)}, bf16[2,128,8,2,128]{1,4,3,2,0:T(8,128)(2,1)}) fusion(f32[2,128,8,2]{1,3,2,0:T(2,128)S(1)} %bitcast.339, f32[2,8,128,2,128]{4,2,3,1,0:T(8,128)S(1)} %fusion.23, f32[2,8,128,2,128]{4,2,3,1,0:T(8,128)S(1)} %fusion.25, f32[2,8,128,128,2]{3,2,4,1,0:T(8,128)S(1)} %copy-done.29, ...), kind=kOutput, calls=%fused_computation.87 | convolution fusion | flops 137887744 | bytes 10010624 | tf_op jit(solution)/shard_map/xhrij,xjhd->xihrd/dot_general | solution.py:59
  56.6 4.2 %copy.285 = f32[2,8,2,128,128]{4,2,1,3,0:T(2,128)} copy(f32[2,8,2,128,128]{3,4,2,1,0:T(8,128)} %get-tuple-element.90) | data formatting | bytes 4194304
  60.8 5.1 %multiply_reduce_fusion = f32[2,8,2,128]{2,1,3,0:T(8,128)} fusion(f32[2,8,2,128,128]{4,2,1,3,0:T(2,128)} %copy.285, bf16[2,128,8,2,128]{4,3,2,1,0:T(2,128)(2,1)} %reshape.655), kind=kLoop, calls=%fused_computation.40 | loop fusion | flops 1568768 | bytes 3162112
  65.9 2.2 copy.286
  68.1 2.5 %fusion.49 = f32[2,8,128,128,1]{2,3,4,1,0:T(8,128)S(1)} fusion(bf16[2,128,8,2,128]{1,4,3,2,0:T(8,128)(2,1)} %copy.247, f32[2,8,128,128,2]{3,2,4,1,0:T(8,128)} %copy-done.13, f32[2,8,2,128]{3,2,1,0:T(2,128)} %bitcast.340, pred[2,128,128]{1,2,0:T(8,128)(4,1)} %get-tuple-element.69), kind=kOutput, calls=%fused_computation.97 | convolution fusion | flops 135790592 | bytes 4243456 | tf_op jit(solution)/shard_map/xhrij,xihrd->xjhd/dot_general | solution.py:80
  75.7 2.1 collective-permute-start.5
  80.8 11.8 %collective-permute-done.5 = f32[2,128,1024]{1,2,0:T(8,128)S(1)} collective-permute-done((f32[2,128,1024]{1,2,0:T(8,128)S(1)}, f32[2,128,1024]{1,2,0:T(8,128)S(1)}, u32[]{:S(2)}, u32[]{:S(2)}) %collective-permute-start.5) | collective-permute-done | bytes 1048608 | tf_op jit(solution)/shard_map/ppermute | solution.py:19
  94.1 1.9 collective-permute-start.4
  96.0 3.6 %collective-permute-start.6 = (f32[2,128,1024]{1,2,0:T(8,128)}, f32[2,128,1024]{1,2,0:T(8,128)}, u32[]{:S(2)}, u32[]{:S(2)}) collective-permute-start(f32[2,128,1024]{1,2,0:T(8,128)} %get-tuple-element.44), channel_id=1, source_target_pairs={{1,0},{2,1},{3,2},{4,3},{5,4},{6,5},{7,6},{8,7},{9,8},{10,9},{11,1... | collective-permute-start | bytes 3145736 | tf_op jit(solution)/shard_map/ppermute | solution.py:19
  101.1 3.3 %copy.325 = f32[2,128,16,64]{3,2,1,0:T(8,128)} copy(f32[2,128,16,64]{1,3,2,0:T(8,128)} %get-tuple-element.58) | data formatting | bytes 2097152
  104.4 3.3 %copy.326 = f32[2,128,16,64]{3,2,1,0:T(8,128)} copy(f32[2,128,16,64]{1,3,2,0:T(8,128)} %get-tuple-element.59) | data formatting | bytes 2097152
  107.7 1.9 fusion.89
  112.5 3.0 %fusion.32 = (f32[1,2,128,1024]{2,3,1,0:T(8,128)S(1)}, f32[2,128,1024]{1,2,0:T(8,128)}) fusion(f32[2,1,128,1024]{2,3,1,0:T(8,128)S(1)} %bitcast.301, f32[2,1,128,1024]{2,3,1,0:T(8,128)S(1)} %bitcast.319, f32[2,128,1024]{1,2,0:T(8,128)} %collective-permute-done.6, pred[]{:T(512)S(6)} %eq.6, f32[2,1,128,1024]{2,3,1,0:T(8,128)S(1)} %bitcast.323, ...), kind=kLoop, calls=%fused_computation.63 | loop fusion | flops 1572864 | bytes 8388610 | tf_op jit(solution)/shard_map/stack | solution.py:195
  115.5 2.0 collective-permute-start.7
  118.2 2.5 %multiply_reduce_fusion.1 = (f32[128]{0:T(128)}, f32[2,128,16]{2,1,0:T(8,128)}) fusion(f32[2,128,16]{2,1,0:T(8,128)S(1)} %copy.218, f32[2,128,16,64]{3,2,1,0:T(8,128)S(1)} %get-tuple-element.53, f32[2,128,16,64]{3,2,1,0:T(8,128)S(1)} %get-tuple-element.52, f32[128]{0:T(128)S(1)} %copy-done.60, f32[2,128,16,128]{3,2,1,0:T(8,128)S(1)} %bitcast.299), kind=kLoop, calls=%fused_computation.41 | loop fusion | flops 3665792 | bytes 4228096 | tf_op jit(solution)/shard_map/transpose(jvp())/reduce_sum | solution.py:30
  120.7 1.6 copy.242
  125.1 4.8 %fusion = bf16[2,128,16,128]{3,2,1,0:T(8,128)(2,1)} fusion(f32[2,128,16]{2,1,0:T(8,128)} %copy.243, f32[128]{0:T(128)} %param.11, f32[2,128,16]{2,1,0:T(8,128)S(1)} %copy.218, f32[2,128,16,64]{3,2,1,0:T(8,128)} %copy-done.1, f32[2,128,16,64]{3,2,1,0:T(8,128)} %copy-done, f32[2,128,16,128]{3,2,1,0:T(8,128)S(1)} %bitcast.300), kind=kLoop, calls=%fused_computation.1 | loop fusion | flops 3670016 | bytes 5276160 | tf_op jit(solution)/shard_map/convert_element_type | solution.py:203
  129.9 2.4 %convert_element_type.84 = bf16[2,128,2048]{2,1,0:T(8,128)(2,1)} reshape(bf16[2,128,16,128]{3,2,1,0:T(8,128)(2,1)} %fusion) | data formatting | bytes 2097152 | tf_op jit(solution)/shard_map/convert_element_type | solution.py:203
  139.0 1.6 multiply_add_fusion.4
  143.9 91.0 %all-reduce.4 = (f32[128]{0:T(128)}, f32[128]{0:T(128)}) all-reduce(f32[128]{0:T(128)S(1)} %copy-done.72, f32[128]{0:T(128)S(1)} %get-tuple-element.38), channel_id=1, replica_groups=mesh['dp'=4,'ctx'=64] {'dp','ctx'}, use_global_device_ids=true, to_apply=%region_8.9 | all-reduce | flops 256 | bytes 2048 | tf_op jit(solution)/shard_map/psum | solution.py:200
  (216 shorter events, 47.2 us)
Async XLA Ops:
  0.6 4.8 %copy-start.61 = (f32[128]{0:T(128)S(1)}, f32[128]{0:T(128)}, u32[]{:S(2)}) copy-start(f32[128]{0:T(128)} %param.12) | copy-start | bytes 1540
  6.5 7.1 %copy-start.8 = (bf16[2,128,8,128]{3,1,2,0:T(8,128)(2,1)}, bf16[2,128,8,128]{3,1,2,0:T(8,128)(2,1)S(1)}, u32[]{:S(2)}) copy-start(bf16[2,128,8,128]{3,1,2,0:T(8,128)(2,1)S(1)} %maximum_convert_fusion) | copy-start | bytes 1572868
  7.2 6.3 %copy-start.19 = (bf16[2,128,8,128]{1,3,2,0:T(8,128)(2,1)}, bf16[2,128,8,128]{1,3,2,0:T(8,128)(2,1)S(1)}, u32[]{:S(2)}) copy-start(bf16[2,128,8,128]{1,3,2,0:T(8,128)(2,1)S(1)} %copy.223) | copy-start | bytes 1572868
  7.5 6.1 %copy-start.21 = (bf16[2,128,1024]{1,2,0:T(8,128)(2,1)}, bf16[2,128,1024]{1,2,0:T(8,128)(2,1)S(1)}, u32[]{:S(2)}) copy-start(bf16[2,128,1024]{1,2,0:T(8,128)(2,1)S(1)} %copy.224) | copy-start | bytes 1572868
  8.4 17.0 %collective-permute-start.1 = (bf16[2,128,1024]{1,2,0:T(8,128)(2,1)}, bf16[2,128,1024]{1,2,0:T(8,128)(2,1)}, u32[]{:S(2)}, u32[]{:S(2)}) collective-permute-start(bf16[2,128,1024]{1,2,0:T(8,128)(2,1)} %fusion.65), channel_id=1, source_target_pairs={{1,0},{2,1},{3,2},{4,3},{5,4},{6,5},{7,6},{8,7},{9,8},{10,9},{11,1... | collective-permute-start | bytes 1572872 | tf_op jit(solution)/shard_map/ppermute | solution.py:19
  21.4 3.1 %copy-start.63 = (pred[2]{0:T(512)(128)(4,1)S(1)}, pred[2]{0:T(512)(128)(4,1)}, u32[]{:S(2)}) copy-start(pred[2]{0:T(512)(128)(4,1)} %get-tuple-element.78) | copy-start | bytes 10
  21.4 3.1 %copy-start.64 = (pred[2]{0:T(512)(128)(4,1)S(1)}, pred[2]{0:T(512)(128)(4,1)}, u32[]{:S(2)}) copy-start(pred[2]{0:T(512)(128)(4,1)} %get-tuple-element.79) | copy-start | bytes 10
  21.4 3.1 %copy-start.65 = (pred[2]{0:T(512)(128)(4,1)S(1)}, pred[2]{0:T(512)(128)(4,1)}, u32[]{:S(2)}) copy-start(pred[2]{0:T(512)(128)(4,1)} %get-tuple-element.80) | copy-start | bytes 10
  21.4 3.1 %copy-start.66 = (pred[2]{0:T(512)(128)(4,1)S(1)}, pred[2]{0:T(512)(128)(4,1)}, u32[]{:S(2)}) copy-start(pred[2]{0:T(512)(128)(4,1)} %get-tuple-element.81) | copy-start | bytes 10
  21.4 3.1 %copy-start.67 = (s32[2]{0:T(128)S(1)}, s32[2]{0:T(128)}, u32[]{:S(2)}) copy-start(s32[2]{0:T(128)} %get-tuple-element.46) | copy-start | bytes 28
  21.5 3.1 %copy-start.58 = (s32[2,128]{1,0:T(2,128)S(1)}, s32[2,128]{1,0:T(2,128)}, u32[]{:S(2)}) copy-start(s32[2,128]{1,0:T(2,128)} %get-tuple-element.51) | copy-start | bytes 3076
  21.5 3.1 %copy-start.71 = (s32[2,128]{1,0:T(2,128)S(1)}, s32[2,128]{1,0:T(2,128)}, u32[]{:S(2)}) copy-start(s32[2,128]{1,0:T(2,128)} %param.10) | copy-start | bytes 3076
  21.5 3.9 %copy-start.20 = (bf16[2,128,8,128]{1,3,2,0:T(8,128)(2,1)S(1)}, bf16[2,128,8,128]{1,3,2,0:T(8,128)(2,1)}, u32[]{:S(2)}) copy-start(bf16[2,128,8,128]{1,3,2,0:T(8,128)(2,1)} %copy-done.19) | copy-start | bytes 1572868
  21.5 3.9 %copy-start.22 = (bf16[2,128,1024]{1,2,0:T(8,128)(2,1)S(1)}, bf16[2,128,1024]{1,2,0:T(8,128)(2,1)}, u32[]{:S(2)}) copy-start(bf16[2,128,1024]{1,2,0:T(8,128)(2,1)} %copy-done.21) | copy-start | bytes 1572868
  24.4 5.0 %copy-start.9 = (bf16[2,128,8,128]{3,1,2,0:T(8,128)(2,1)S(1)}, bf16[2,128,8,128]{3,1,2,0:T(8,128)(2,1)}, u32[]{:S(2)}) copy-start(bf16[2,128,8,128]{3,1,2,0:T(8,128)(2,1)} %copy-done.8) | copy-start | bytes 1572868
  25.4 6.4 %copy-start.49 = (pred[2,128,128]{1,2,0:T(8,128)(4,1)}, pred[2,128,128]{1,2,0:T(8,128)(4,1)S(1)}, u32[]{:S(2)}) copy-start(pred[2,128,128]{1,2,0:T(8,128)(4,1)S(1)} %get-tuple-element.68) | copy-start | bytes 98308
  27.5 14.6 %collective-permute-start = (bf16[2,128,1024]{1,2,0:T(8,128)(2,1)}, bf16[2,128,1024]{1,2,0:T(8,128)(2,1)}, u32[]{:S(2)}, u32[]{:S(2)}) collective-permute-start(bf16[2,128,1024]{1,2,0:T(8,128)(2,1)} %get-tuple-element.49), channel_id=1, source_target_pairs={{0,1},{1,2},{2,3},{3,4},{4,5},{5,6},{6,7},{7,8},{8,9},{9,10},{10,1... | collective-permute-start | bytes 1572872 | tf_op jit(solution)/shard_map/ppermute | solution.py:19
  31.8 14.9 %collective-permute-start.3 = (bf16[2,128,1024]{1,2,0:T(8,128)(2,1)}, bf16[2,128,1024]{1,2,0:T(8,128)(2,1)}, u32[]{:S(2)}, u32[]{:S(2)}) collective-permute-start(bf16[2,128,1024]{1,2,0:T(8,128)(2,1)} %get-tuple-element.48), channel_id=1, source_target_pairs={{1,0},{2,1},{3,2},{4,3},{5,4},{6,5},{7,6},{8,7},{9,8},{10,9},{11,1... | collective-permute-start | bytes 1572872 | tf_op jit(solution)/shard_map/ppermute | solution.py:19
  42.1 4.0 %copy-start.43 = (pred[2,128,128]{1,2,0:T(8,128)(4,1)S(1)}, pred[2,128,128]{1,2,0:T(8,128)(4,1)}, u32[]{:S(2)}) copy-start(pred[2,128,128]{1,2,0:T(8,128)(4,1)} %get-tuple-element.70) | copy-start | bytes 98308
  42.1 8.9 %collective-permute-start.2 = (bf16[2,128,1024]{1,2,0:T(8,128)(2,1)}, bf16[2,128,1024]{1,2,0:T(8,128)(2,1)S(1)}, u32[]{:S(2)}, u32[]{:S(2)}) collective-permute-start(bf16[2,128,1024]{1,2,0:T(8,128)(2,1)} %collective-permute-done), channel_id=1, source_target_pairs={{0,1},{1,2},{2,3},{3,4},{4,5},{5,6},{6,7},{7,8},{8,9},{9,10},{10,1... | collective-permute-start | bytes 1572872 | tf_op jit(solution)/shard_map/ppermute | solution.py:19
  53.1 3.5 %copy-start.56 = (f32[2,2,8,128]{3,2,1,0:T(8,128)}, f32[2,2,8,128]{3,2,1,0:T(8,128)S(1)}, u32[]{:S(2)}) copy-start(f32[2,2,8,128]{3,2,1,0:T(8,128)S(1)} %add_add_fusion.2) | copy-start | bytes 49156
  75.1 3.1 %copy-start.26 = (bf16[2,8,2,128,128]{3,4,2,1,0:T(8,128)(2,1)}, bf16[2,8,2,128,128]{3,4,2,1,0:T(8,128)(2,1)S(1)}, u32[]{:S(2)}) copy-start(bf16[2,8,2,128,128]{3,4,2,1,0:T(8,128)(2,1)S(1)} %fusion.5) | copy-start | bytes 3145732
  75.7 16.9 %collective-permute-start.5 = (f32[2,128,1024]{1,2,0:T(8,128)S(1)}, f32[2,128,1024]{1,2,0:T(8,128)S(1)}, u32[]{:S(2)}, u32[]{:S(2)}) collective-permute-start(f32[2,128,1024]{1,2,0:T(8,128)S(1)} %fusion.44), channel_id=1, source_target_pairs={{1,0},{2,1},{3,2},{4,3},{5,4},{6,5},{7,6},{8,7},{9,8},{10,9},{11,1... | collective-permute-start | bytes 3145736 | tf_op jit(solution)/shard_map/ppermute | solution.py:19
  79.8 12.9 %copy-start.6 = (f32[2,8,128,128,1]{3,2,4,1,0:T(8,128)}, f32[2,8,128,128,1]{3,2,4,1,0:T(8,128)S(1)}, u32[]{:S(2)}) copy-start(f32[2,8,128,128,1]{3,2,4,1,0:T(8,128)S(1)} %fusion.88) | copy-start | bytes 3145732
  80.8 13.3 %copy-start.27 = (f32[2,8,128,128,1]{2,3,4,1,0:T(8,128)}, f32[2,8,128,128,1]{2,3,4,1,0:T(8,128)S(1)}, u32[]{:S(2)}) copy-start(f32[2,8,128,128,1]{2,3,4,1,0:T(8,128)S(1)} %fusion.47) | copy-start | bytes 3145732
  94.1 17.3 %collective-permute-start.4 = (f32[2,128,1024]{1,2,0:T(8,128)}, f32[2,128,1024]{1,2,0:T(8,128)}, u32[]{:S(2)}, u32[]{:S(2)}) collective-permute-start(f32[2,128,1024]{1,2,0:T(8,128)} %get-tuple-element.45), channel_id=1, source_target_pairs={{0,1},{1,2},{2,3},{3,4},{4,5},{5,6},{6,7},{7,8},{8,9},{9,10},{10,1... | collective-permute-start | bytes 3145736 | tf_op jit(solution)/shard_map/ppermute | solution.py:19
  96.0 16.4 %collective-permute-start.6 = (f32[2,128,1024]{1,2,0:T(8,128)}, f32[2,128,1024]{1,2,0:T(8,128)}, u32[]{:S(2)}, u32[]{:S(2)}) collective-permute-start(f32[2,128,1024]{1,2,0:T(8,128)} %get-tuple-element.44), channel_id=1, source_target_pairs={{1,0},{2,1},{3,2},{4,3},{5,4},{6,5},{7,6},{8,7},{9,8},{10,9},{11,1... | collective-permute-start | bytes 3145736 | tf_op jit(solution)/shard_map/ppermute | solution.py:19
  111.3 4.2 %copy-start.25 = (f32[2,8,128,128,1]{2,3,4,1,0:T(8,128)}, f32[2,8,128,128,1]{2,3,4,1,0:T(8,128)S(1)}, u32[]{:S(2)}) copy-start(f32[2,8,128,128,1]{2,3,4,1,0:T(8,128)S(1)} %fusion.45) | copy-start | bytes 3145732
  112.4 5.1 %copy-start.15 = (f32[2,128,16,64]{3,2,1,0:T(8,128)S(1)}, f32[2,128,16,64]{3,2,1,0:T(8,128)}, u32[]{:S(2)}) copy-start(f32[2,128,16,64]{3,2,1,0:T(8,128)} %copy.325) | copy-start | bytes 3145732
  112.5 5.1 %copy-start.16 = (f32[2,128,16,64]{3,2,1,0:T(8,128)S(1)}, f32[2,128,16,64]{3,2,1,0:T(8,128)}, u32[]{:S(2)}) copy-start(f32[2,128,16,64]{3,2,1,0:T(8,128)} %copy.326) | copy-start | bytes 3145732
  115.5 18.2 %collective-permute-start.7 = (f32[2,128,1024]{1,2,0:T(8,128)}, f32[2,128,1024]{1,2,0:T(8,128)}, u32[]{:S(2)}, u32[]{:S(2)}) collective-permute-start(f32[2,128,1024]{1,2,0:T(8,128)} %get-tuple-element.43), channel_id=1, source_target_pairs={{0,1},{1,2},{2,3},{3,4},{4,5},{5,6},{6,7},{7,8},{8,9},{9,10},{10,1... | collective-permute-start | bytes 3145736 | tf_op jit(solution)/shard_map/ppermute | solution.py:19
  129.9 3.8 %copy-start.5 = (f32[2,8,128,128,1]{3,2,4,1,0:T(8,128)S(1)}, f32[2,8,128,128,1]{3,2,4,1,0:T(8,128)}, u32[]{:S(2)}) copy-start(f32[2,8,128,128,1]{3,2,4,1,0:T(8,128)} %copy-done.4) | copy-start | bytes 3145732
  (49 other events, 103.0 us)
where the time goes:
time: 236 us; the launch traced here: 235 us
  blocking collectives  91 us (39%)
  local copies, waits for them, and re-layouts  45.8 us (19%)
  other arithmetic  40.8 us (17%)
  starting transfers between devices  22.5 us (10%)
  matrix products  17.9 us (8%)
  waiting for transfers between devices  15.2 us (6%)
    psum x1, blocking collectives, shards(): lax.psum((grad_gain_q, grad_gain_k), ('dp', 'ctx'))  91 us
    unnamed x158, local copies, waits for them, and re-layouts  24.7 us
    ppermute x8, starting transfers between devices, from_behind(): return lax.ppermute(block, axis, route)  22.5 us
    ppermute x8, waiting for transfers between devices, from_behind(): return lax.ppermute(block, axis, route)  15.2 us
    reshape x2, local copies, waits for them, and re-layouts, shards(): cotangent_heads = cotangent.reshape(2, block, kv_heads, repeat, head_width)  6.23 us
    unnamed x1, other arithmetic  5.11 us
    convert_element_type x1, other arithmetic, shards(): grad_queries.reshape(2, block, -1).astype(jnp.bfloat16)  4.83 us
  transfers between devices with their start and end apart: 8, of which 3 were waited for; matrix products, arithmetic and copies ran while one was open for 23% of the time, Pallas kernels for 0%

commit v1 on v0

v1 whole, which is shorter than its diff:
```python
import functools

import jax
import jax.numpy as jnp
from jax import lax
from jax.experimental import pallas as pl
from jax.experimental.pallas import tpu as pltpu
from jax.sharding import PartitionSpec as P

query_factor = 168.0 ** (-0.5)
rotary_base = 1000000.0
norm_epsilon = 1e-06
PANELS = 3
F32 = jnp.float32
BF16 = jnp.bfloat16


def rotary_angles(position, head_width):
    exponent = jnp.arange(head_width // 2, dtype=F32) * (2.0 / head_width)
    frequency = jnp.exp(-exponent * jnp.log(F32(rotary_base)))
    return position.astype(F32)[..., None] * frequency


def slot_positions(slot, rows, group, block):
    ascending = slot * block + rows
    descending = slot * block + block - 1 - rows
    inside = (slot >= 0) & (slot < 2 * group)
    return jnp.where(inside, jnp.where(slot < group, ascending, descending), -1)


def half_turn(x):
    return pltpu.roll(x, x.shape[-1] // 2, 1)


def normalize(x):
    inverse = lax.rsqrt(jnp.mean(x * x, axis=-1, keepdims=True) + norm_epsilon)
    return x * inverse, inverse


def rotate(y, cosine, sine):
    return y * cosine + half_turn(y) * sine


def unrotate(g, cosine, sine):
    return g * cosine + half_turn(g * sine)


def norm_back(grad, normed, inverse):
    return inverse * (grad - normed * jnp.mean(grad * normed, axis=-1, keepdims=True))


def contract(a, b, da, db):
    return lax.dot_general(a, b, (((da,), (db,)), ((), ())), preferred_element_type=F32)


def attend_kernel(
    group,
    index_ref,
    doc_ref,
    gain_q_ref,
    gain_k_ref,
    cos_ref,
    sin_ref,
    q_ref,
    k_ref,
    v_ref,
    c_ref,
    lo1_ref,
    hi1_ref,
    lo2_ref,
    hi2_ref,
    att_ref,
    gq_ref,
    own_k_ref,
    own_v_ref,
    lo1_out,
    hi1_out,
    lo2_out,
    hi2_out,
    gains_ref,
    mask_ref,
):
    step = pl.program_id(0)
    block = q_ref.shape[1]
    width = k_ref.shape[2]
    repeat = q_ref.shape[2] // width
    device = index_ref[0]

    @pl.when(step == 0)
    def _():
        gains_ref[...] = jnp.zeros_like(gains_ref)
        for x in range(2):
            slot = device if x == 0 else 2 * group - 1 - device
            lane = lax.broadcasted_iota(jnp.int32, (block, block), 1)
            row = lax.broadcasted_iota(jnp.int32, (block, block), 0)
            query_position = slot * block + (lane if x == 0 else block - 1 - lane)
            for panel in range(PANELS):
                seen = slot - panel
                upward = seen < group
                key_position = (
                    seen * block
                    + jnp.where(upward, 0, block - 1)
                    + jnp.where(upward, 1, -1) * row
                )
                key_position = jnp.where(seen >= 0, key_position, -1)
                allowed = (doc_ref[x : x + 1, :] <= key_position) & (key_position <= query_position)
                value = jnp.where(allowed, 1.0, 0.0).astype(F32)
                for r in range(repeat):
                    mask_ref[
                        x, panel * block : (panel + 1) * block, r * block : (r + 1) * block
                    ] = value

    gain_q = gain_q_ref[...] * query_factor
    gain_k = gain_k_ref[...]
    near = (lo1_ref, hi1_ref)
    far = (lo2_ref, hi2_ref)
    near_out = (lo1_out, hi1_out)
    far_out = (lo2_out, hi2_out)
    sum_q = jnp.zeros((1, width), F32)
    sum_k = jnp.zeros((1, width), F32)
    for x in range(2):
        cos_q = cos_ref[x, 0]
        sin_q = sin_ref[x, 0]
        q_parts, q_normed, q_inverse, c_parts = [], [], [], []
        for r in range(repeat):
            normed, inverse = normalize(q_ref[x, :, r * width : (r + 1) * width].astype(F32))
            q_normed.append(normed)
            q_inverse.append(inverse)
            q_parts.append(rotate(normed * gain_q, cos_q, sin_q).astype(BF16))
            c_parts.append(c_ref[x, :, r * width : (r + 1) * width])
        q_rot = jnp.concatenate(q_parts, axis=0)
        cot = jnp.concatenate(c_parts, axis=0)
        raw_k = (k_ref[x], near[x][0], far[x][0])
        k_parts, k_normed, k_inverse = [], [], []
        for panel in range(PANELS):
            normed, inverse = normalize(raw_k[panel].astype(F32))
            k_normed.append(normed)
            k_inverse.append(inverse)
            k_parts.append(
                rotate(normed * gain_k, cos_ref[x, panel], sin_ref[x, panel]).astype(BF16)
            )
        k_rot = jnp.concatenate(k_parts, axis=0)
        vals = jnp.concatenate([v_ref[x], near[x][1], far[x][1]], axis=0)
        expo = jnp.exp(contract(k_rot, q_rot, 1, 1)) * mask_ref[x]
        dprob = contract(vals, cot, 1, 1)
        inverse_total = 1.0 / jnp.sum(expo, axis=0, keepdims=True)
        probs = expo * inverse_total
        delta = jnp.sum(probs * dprob, axis=0, keepdims=True)
        dscore = (probs * (dprob - delta)).astype(BF16)
        probs = probs.astype(BF16)
        attended = contract(probs, vals, 0, 0)
        grad_q = contract(dscore, k_rot, 0, 0)
        grad_v = contract(probs, cot, 1, 0)
        grad_k = contract(dscore, q_rot, 1, 0)
        for r in range(repeat):
            rows = slice(r * block, (r + 1) * block)
            cols = slice(r * width, (r + 1) * width)
            att_ref[x, :, cols] = attended[rows].astype(BF16)
            back = unrotate(grad_q[rows], cos_q, sin_q)
            sum_q = sum_q + jnp.sum(back * q_normed[r], axis=0, keepdims=True)
            gq_ref[x, :, cols] = norm_back(back * gain_q, q_normed[r], q_inverse[r]).astype(BF16)
        for panel in range(PANELS):
            rows = slice(panel * block, (panel + 1) * block)
            back = unrotate(grad_k[rows], cos_ref[x, panel], sin_ref[x, panel])
            sum_k = sum_k + jnp.sum(back * k_normed[panel], axis=0, keepdims=True)
            raw = norm_back(back * gain_k, k_normed[panel], k_inverse[panel])
            if panel == 0:
                own_k_ref[x] = raw
                own_v_ref[x] = grad_v[rows]
            else:
                target = near_out[x] if panel == 1 else far_out[x]
                target[0] = raw.astype(BF16)
                target[1] = grad_v[rows].astype(BF16)
    gains_ref[0:1, :] += sum_q * query_factor
    gains_ref[1:2, :] += sum_k


def attend(group, device, doc_start, gain_q, gain_k, cosine, sine, queries, keys, values, cotangent, panels):
    block = queries.shape[1]
    width = gain_q.shape[0]
    heads = keys.shape[2] // width
    repeat = queries.shape[2] // keys.shape[2]
    whole = lambda shape: pl.BlockSpec(shape, lambda h: (0,) * len(shape))
    wide = pl.BlockSpec((2, block, repeat * width), lambda h: (0, 0, h))
    slim = pl.BlockSpec((2, block, width), lambda h: (0, 0, h))
    pair = jax.ShapeDtypeStruct((2, block, heads * width), BF16)
    pairs = 2 * heads * block * repeat * block * PANELS * width
    return pl.pallas_call(
        functools.partial(attend_kernel, group),
        grid=(heads,),
        in_specs=[
            pl.BlockSpec(memory_space=pltpu.SMEM),
            whole((2, block)),
            whole((1, width)),
            whole((1, width)),
            whole((2, PANELS, block, width)),
            whole((2, PANELS, block, width)),
            wide,
            slim,
            slim,
            wide,
            slim,
            slim,
            slim,
            slim,
        ],
        out_specs=[wide, wide, slim, slim, slim, slim, slim, slim, whole((2, width))],
        out_shape=[
            jax.ShapeDtypeStruct(queries.shape, BF16),
            jax.ShapeDtypeStruct(queries.shape, BF16),
            jax.ShapeDtypeStruct(keys.shape, F32),
            jax.ShapeDtypeStruct(keys.shape, F32),
            pair,
            pair,
            pair,
            pair,
            jax.ShapeDtypeStruct((2, width), F32),
        ],
        scratch_shapes=[pltpu.VMEM((2, PANELS * block, repeat * block), F32)],
        compiler_params=pltpu.CompilerParams(
            dimension_semantics=("arbitrary",), vmem_limit_bytes=40 * 1024 * 1024
        ),
        cost_estimate=pl.CostEstimate(
            flops=12 * pairs, bytes_accessed=12 * 1024 * 1024, transcendentals=pairs // width
        ),
        name="attend",
    )(device, doc_start, gain_q[None], gain_k[None], cosine, sine, queries, keys, values, cotangent, *panels)


def total_over(x, axis):
    size = lax.axis_size(axis)
    distance = 1
    while distance < size:
        x = x + lax.ppermute(x, axis, [(i, i ^ distance) for i in range(size)])
        distance *= 2
    return x


def shards(queries, keys, values, doc_start, gain_q, key_norm_gain, cotangent):
    group = lax.axis_size("ctx")
    block = queries.shape[1]
    width = gain_q.shape[0]
    device = lax.axis_index("ctx")
    at_fold = device == group - 1
    upward = [(i, i + 1) for i in range(group - 1)]
    downward = [(i + 1, i) for i in range(group - 1)]
    up = lambda a: lax.ppermute(a, "ctx", upward)
    down = lambda a: lax.ppermute(a, "ctx", downward)

    low = jnp.stack([keys[0], values[0]])
    high = jnp.stack([keys[1], values[1]])
    low1 = up(low)
    high1 = jnp.where(at_fold, low, down(high))
    low2 = up(low1)
    high2 = down(high1)
    high2 = jnp.where(at_fold, low1, high2)

    rows = jnp.arange(block, dtype=jnp.int32)
    slots = jnp.stack([device, 2 * group - 1 - device])[:, None] - jnp.arange(PANELS)[None, :]
    angle = rotary_angles(slot_positions(slots[..., None], rows, group, block), width)
    cosine = jnp.cos(angle)
    sine = jnp.sin(angle)
    cosine = jnp.concatenate([cosine, cosine], axis=-1)
    sine = jnp.concatenate([-sine, sine], axis=-1)

    attended, grad_queries, own_k, own_v, low1_g, high1_g, low2_g, high2_g, gains = attend(
        group,
        device[None].astype(jnp.int32),
        doc_start,
        gain_q,
        key_norm_gain,
        cosine,
        sine,
        queries,
        keys,
        values,
        cotangent,
        (low1, high1, low2, high2),
    )
    back_low = jnp.where(at_fold, high2_g, down(low2_g))
    back_high = up(high2_g)
    back_low = (back_low.astype(F32) + low1_g.astype(F32)).astype(BF16)
    back_high = (back_high.astype(F32) + high1_g.astype(F32)).astype(BF16)
    home_low = jnp.where(at_fold, back_high, down(back_low))
    home_high = up(back_high)
    gains = total_over(total_over(gains, "ctx"), "dp")
    home = jnp.stack([home_low, home_high], axis=1).astype(F32)
    grad_keys = (own_k + home[0]).astype(BF16)
    grad_values = (own_v + home[1]).astype(BF16)
    return attended, grad_queries, grad_keys, grad_values, gains[0], gains[1]


def solution(mesh):
    tokens = P(None, ("dp", "ctx"), None)
    return jax.shard_map(
        shards,
        mesh=mesh,
        in_specs=(tokens, tokens, tokens, P(None, ("dp", "ctx")), P(), P(), tokens),
        out_specs=(tokens, tokens, tokens, tokens, P(), P()),
        check_vma=False,
    )
```

time: 236 us -> 131 us (0.56)
  the two profiles are of different devices: /device:TPU:1 before, /device:TPU:62 now
where the time goes in v1:
time: 131 us
  waiting for transfers between devices  51.8 us (40%)
  starting transfers between devices  46.4 us (35%)
  Pallas kernels  25.6 us (20%)
  other arithmetic  4.24 us (3%)
  local copies, waits for them, and re-layouts  1.85 us (1%)
    ppermute x8, waiting for transfers between devices, total_over(): x = x + lax.ppermute(x, axis, [(i, i ^ distance) for i in range(size)])  27.9 us
    pallas_call x1, Pallas kernels, attend(): pl.pallas_call(functools.partial(attend_kernel, group), grid=(heads,), in...  25.6 us
    ppermute x4, starting transfers between devices, shards(): up = lambda a: lax.ppermute(a, 'ctx', upward)  24.7 us
    ppermute x4, waiting for transfers between devices, shards(): down = lambda a: lax.ppermute(a, 'ctx', downward)  15.2 us
    ppermute x8, starting transfers between devices, total_over(): x = x + lax.ppermute(x, axis, [(i, i ^ distance) for i in range(size)])  11.7 us
    ppermute x4, starting transfers between devices, shards(): down = lambda a: lax.ppermute(a, 'ctx', downward)  10 us
    ppermute x4, waiting for transfers between devices, shards(): up = lambda a: lax.ppermute(a, 'ctx', upward)  8.68 us
  transfers between devices with their start and end apart: 16, of which 13 were waited for; matrix products, arithmetic and copies ran while one was open for 2% of the time, Pallas kernels for 0%

profile of v1, /device:TPU:62, one launch (start us, length us, event | category | flops | bytes accessed | tf_op | source)
XLA Modules:
  0.0 130.7 jit_solution(5926675464636018699)
XLA Ops:
  0.6 1.3 fusion.7
  2.0 2.1 %collective-permute-start.1 = (bf16[2,128,1024]{2,1,0:T(8,128)(2,1)S(1)}, bf16[2,128,1024]{2,1,0:T(8,128)(2,1)S(1)}, u32[]{:S(2)}, u32[]{:S(2)}) collective-permute-start(bf16[2,128,1024]{2,1,0:T(8,128)(2,1)S(1)} %pad_maximum_fusion.1), channel_id=1, source_target_pairs={{1,0},{2,1},{3,2},{4,3},{5,4},{6,5},{7,6},{8,7},{9,8},{10,9},{11,1... | collective-permute-start | bytes 1572872 | tf_op jit(solution)/shard_map/ppermute | solution.py:248
  4.2 6.5 %collective-permute-done.1 = bf16[2,128,1024]{2,1,0:T(8,128)(2,1)S(1)} collective-permute-done((bf16[2,128,1024]{2,1,0:T(8,128)(2,1)S(1)}, bf16[2,128,1024]{2,1,0:T(8,128)(2,1)S(1)}, u32[]{:S(2)}, u32[]{:S(2)}) %collective-permute-start.1) | collective-permute-done | bytes 524320 | tf_op jit(solution)/shard_map/ppermute | solution.py:248
  10.8 5.6 %collective-permute-start = (bf16[2,128,1024]{2,1,0:T(8,128)(2,1)S(1)}, bf16[2,128,1024]{2,1,0:T(8,128)(2,1)S(1)}, u32[]{:S(2)}, u32[]{:S(2)}) collective-permute-start(bf16[2,128,1024]{2,1,0:T(8,128)(2,1)S(1)} %get-tuple-element.29), channel_id=1, source_target_pairs={{0,1},{1,2},{2,3},{3,4},{4,5},{5,6},{6,7},{7,8},{8,9},{9,10},{10,1... | collective-permute-start | bytes 1572872 | tf_op jit(solution)/shard_map/ppermute | solution.py:247
  16.5 1.9 %collective-permute-start.3 = (bf16[2,128,1024]{2,1,0:T(8,128)(2,1)S(1)}, bf16[2,128,1024]{2,1,0:T(8,128)(2,1)S(1)}, u32[]{:S(2)}, u32[]{:S(2)}) collective-permute-start(bf16[2,128,1024]{2,1,0:T(8,128)(2,1)S(1)} %get-tuple-element.28.hi1_ref), channel_id=1, source_target_pairs={{1,0},{2,1},{3,2},{4,3},{5,4},{6,5},{7,6},{8,7},{9,8},{10,9},{11,1... | collective-permute-start | bytes 1572872 | tf_op jit(solution)/shard_map/ppermute | solution.py:248
  18.6 2.9 %collective-permute-done.lo1_ref = bf16[2,128,1024]{2,1,0:T(8,128)(2,1)S(1)} collective-permute-done((bf16[2,128,1024]{2,1,0:T(8,128)(2,1)S(1)}, bf16[2,128,1024]{2,1,0:T(8,128)(2,1)S(1)}, u32[]{:S(2)}, u32[]{:S(2)}) %collective-permute-start) | collective-permute-done | bytes 524320 | tf_op jit(solution)/shard_map/ppermute | solution.py:247
  21.5 2.9 %collective-permute-start.2 = (bf16[2,128,1024]{2,1,0:T(8,128)(2,1)S(1)}, bf16[2,128,1024]{2,1,0:T(8,128)(2,1)S(1)}, u32[]{:S(2)}, u32[]{:S(2)}) collective-permute-start(bf16[2,128,1024]{2,1,0:T(8,128)(2,1)S(1)} %collective-permute-done.lo1_ref), channel_id=1, source_target_pairs={{0,1},{1,2},{2,3},{3,4},{4,5},{5,6},{6,7},{7,8},{8,9},{9,10},{10,1... | collective-permute-start | bytes 1572872 | tf_op jit(solution)/shard_map/ppermute | solution.py:247
  24.4 1.4 %fusion.4 = (f32[2,3,128,64]{3,2,1,0:T(8,128)S(1)}, f32[2,3,128,64]{3,2,1,0:T(8,128)S(1)}, f32[2,3,128,64]{3,2,1,0:T(8,128)S(1)}) fusion(f32[64]{0:T(128)S(1)} %multiply_exponential_fusion, f32[2,3,128]{2,1,0:T(4,128)S(1)} %select_convert_fusion), kind=kLoop, calls=%fused_computation.18 | loop fusion | flops 98304 | bytes 593152 | tf_op jit(solution)/shard_map/neg | solution.py:264
  25.9 0.3 pad_maximum_fusion.2
  26.2 5.8 %collective-permute-done.2.lo2_ref = bf16[2,128,1024]{2,1,0:T(8,128)(2,1)S(1)} collective-permute-done((bf16[2,128,1024]{2,1,0:T(8,128)(2,1)S(1)}, bf16[2,128,1024]{2,1,0:T(8,128)(2,1)S(1)}, u32[]{:S(2)}, u32[]{:S(2)}) %collective-permute-start.2) | collective-permute-done | bytes 524320 | tf_op jit(solution)/shard_map/ppermute | solution.py:247
  32.0 25.6 %attend.1 = (bf16[2,128,2048]{2,1,0:T(8,128)(2,1)}, bf16[2,128,2048]{2,1,0:T(8,128)(2,1)}, f32[2,128,1024]{2,1,0:T(8,128)S(1)}, f32[2,128,1024]{2,1,0:T(8,128)S(...) custom-call(s32[1]{0:T(128)} %bitcast.index_ref, ...), custom_call_target="tpu_custom_call" | custom-call | flops 2415919104 | bytes 12582912 | tf_op jit(solution)/shard_map/attend/pallas_call | solution.py:188
  57.6 1.9 %collective-permute-start.5 = (bf16[2,128,1024]{2,1,0:T(8,128)(2,1)S(1)}, bf16[2,128,1024]{2,1,0:T(8,128)(2,1)S(1)}, u32[]{:S(2)}, u32[]{:S(2)}) collective-permute-start(bf16[2,128,1024]{2,1,0:T(8,128)(2,1)S(1)} %get-tuple-element.20), channel_id=1, source_target_pairs={{1,0},{2,1},{3,2},{4,3},{5,4},{6,5},{7,6},{8,7},{9,8},{10,9},{11,1... | collective-permute-start | bytes 1572872 | tf_op jit(solution)/shard_map/ppermute | solution.py:248
  59.5 5.0 %collective-permute-start.4 = (bf16[2,128,1024]{2,1,0:T(8,128)(2,1)S(1)}, bf16[2,128,1024]{2,1,0:T(8,128)(2,1)S(1)}, u32[]{:S(2)}, u32[]{:S(2)}) collective-permute-start(bf16[2,128,1024]{2,1,0:T(8,128)(2,1)S(1)} %get-tuple-element.18), channel_id=1, source_target_pairs={{0,1},{1,2},{2,3},{3,4},{4,5},{5,6},{6,7},{7,8},{8,9},{9,10},{10,1... | collective-permute-start | bytes 1572872 | tf_op jit(solution)/shard_map/ppermute | solution.py:247
  64.6 1.6 %collective-permute-done.5 = bf16[2,128,1024]{2,1,0:T(8,128)(2,1)S(1)} collective-permute-done((bf16[2,128,1024]{2,1,0:T(8,128)(2,1)S(1)}, bf16[2,128,1024]{2,1,0:T(8,128)(2,1)S(1)}, u32[]{:S(2)}, u32[]{:S(2)}) %collective-permute-start.5) | collective-permute-done | bytes 524320 | tf_op jit(solution)/shard_map/ppermute | solution.py:248
  66.5 4.1 %collective-permute-start.6 = (bf16[2,128,1024]{2,1,0:T(8,128)(2,1)S(1)}, bf16[2,128,1024]{2,1,0:T(8,128)(2,1)S(1)}, u32[]{:S(2)}, u32[]{:S(2)}) collective-permute-start(bf16[2,128,1024]{2,1,0:T(8,128)(2,1)S(1)} %add_convert_fusion), channel_id=1, source_target_pairs={{1,0},{2,1},{3,2},{4,3},{5,4},{6,5},{7,6},{8,7},{9,8},{10,9},{11,1... | collective-permute-start | bytes 1572872 | tf_op jit(solution)/shard_map/ppermute | solution.py:248
  70.6 7.1 %collective-permute-done.6 = bf16[2,128,1024]{2,1,0:T(8,128)(2,1)S(1)} collective-permute-done((bf16[2,128,1024]{2,1,0:T(8,128)(2,1)S(1)}, bf16[2,128,1024]{2,1,0:T(8,128)(2,1)S(1)}, u32[]{:S(2)}, u32[]{:S(2)}) %collective-permute-start.6) | collective-permute-done | bytes 524320 | tf_op jit(solution)/shard_map/ppermute | solution.py:248
  77.7 0.3 select_bitcast_fusion
  78.0 11.2 %collective-permute-start.7 = (bf16[2,128,1024]{2,1,0:T(8,128)(2,1)S(1)}, bf16[2,128,1024]{2,1,0:T(8,128)(2,1)S(1)}, u32[]{:S(2)}, u32[]{:S(2)}) collective-permute-start(bf16[2,128,1024]{2,1,0:T(8,128)(2,1)S(1)} %get-tuple-element.25), channel_id=1, source_target_pairs={{0,1},{1,2},{2,3},{3,4},{4,5},{5,6},{6,7},{7,8},{8,9},{9,10},{10,1... | collective-permute-start | bytes 1572872 | tf_op jit(solution)/shard_map/ppermute | solution.py:247
  89.4 1.4 %collective-permute-done.8 = f32[2,128]{1,0:T(2,128)S(1)} collective-permute-done((f32[2,128]{1,0:T(2,128)S(1)}, f32[2,128]{1,0:T(2,128)S(1)}, u32[]{:S(2)}, u32[]{:S(2)}) %collective-permute-start.8) | collective-permute-done | bytes 1056 | tf_op jit(solution)/shard_map/ppermute | solution.py:234
  90.8 3.6 %collective-permute-done.9 = f32[2,128]{1,0:T(2,128)S(1)} collective-permute-done((f32[2,128]{1,0:T(2,128)S(1)}, f32[2,128]{1,0:T(2,128)S(1)}, u32[]{:S(2)}, u32[]{:S(2)}) %collective-permute-start.9) | collective-permute-done | bytes 1056 | tf_op jit(solution)/shard_map/ppermute | solution.py:234
  94.4 5.1 %collective-permute-done.10 = f32[2,128]{1,0:T(2,128)S(1)} collective-permute-done((f32[2,128]{1,0:T(2,128)S(1)}, f32[2,128]{1,0:T(2,128)S(1)}, u32[]{:S(2)}, u32[]{:S(2)}) %collective-permute-start.10) | collective-permute-done | bytes 1056 | tf_op jit(solution)/shard_map/ppermute | solution.py:234
  99.6 3.5 %collective-permute-done.11 = f32[2,128]{1,0:T(2,128)S(1)} collective-permute-done((f32[2,128]{1,0:T(2,128)S(1)}, f32[2,128]{1,0:T(2,128)S(1)}, u32[]{:S(2)}, u32[]{:S(2)}) %collective-permute-start.11) | collective-permute-done | bytes 1056 | tf_op jit(solution)/shard_map/ppermute | solution.py:234
  103.0 8.1 %collective-permute-start.12 = (f32[2,128]{1,0:T(2,128)S(1)}, f32[2,128]{1,0:T(2,128)S(1)}, u32[]{:S(2)}, u32[]{:S(2)}) collective-permute-start(f32[2,128]{1,0:T(2,128)S(1)} %add.77), channel_id=1, source_target_pairs={{0,16},{1,17},{2,18},{3,19},{4,20},{5,21},{6,22},{7,23},{8,24},{9,... | collective-permute-start | bytes 3080 | tf_op jit(solution)/shard_map/ppermute | solution.py:234
  111.1 1.5 %collective-permute-done.12 = f32[2,128]{1,0:T(2,128)S(1)} collective-permute-done((f32[2,128]{1,0:T(2,128)S(1)}, f32[2,128]{1,0:T(2,128)S(1)}, u32[]{:S(2)}, u32[]{:S(2)}) %collective-permute-start.12) | collective-permute-done | bytes 1056 | tf_op jit(solution)/shard_map/ppermute | solution.py:234
  112.7 1.1 collective-permute-start.13
  113.8 6.4 %collective-permute-done.13 = f32[2,128]{1,0:T(2,128)S(1)} collective-permute-done((f32[2,128]{1,0:T(2,128)S(1)}, f32[2,128]{1,0:T(2,128)S(1)}, u32[]{:S(2)}, u32[]{:S(2)}) %collective-permute-start.13) | collective-permute-done | bytes 1056 | tf_op jit(solution)/shard_map/ppermute | solution.py:234
  120.2 0.8 collective-permute-start.14
  121.0 2.7 %collective-permute-done.14 = f32[2,128]{1,0:T(2,128)S(1)} collective-permute-done((f32[2,128]{1,0:T(2,128)S(1)}, f32[2,128]{1,0:T(2,128)S(1)}, u32[]{:S(2)}, u32[]{:S(2)}) %collective-permute-start.14) | collective-permute-done | bytes 1056 | tf_op jit(solution)/shard_map/ppermute | solution.py:234
  123.7 1.4 %collective-permute-start.15 = (f32[2,128]{1,0:T(2,128)S(1)}, f32[2,128]{1,0:T(2,128)S(1)}, u32[]{:S(2)}, u32[]{:S(2)}) collective-permute-start(f32[2,128]{1,0:T(2,128)S(1)} %add.80), channel_id=1, source_target_pairs={{0,128},{64,192},{128,0},{192,64},{1,129},{65,193},{129,1},{193,65... | collective-permute-start | bytes 3080 | tf_op jit(solution)/shard_map/ppermute | solution.py:234
  125.1 3.7 %collective-permute-done.15 = f32[2,128]{1,0:T(2,128)S(1)} collective-permute-done((f32[2,128]{1,0:T(2,128)S(1)}, f32[2,128]{1,0:T(2,128)S(1)}, u32[]{:S(2)}, u32[]{:S(2)}) %collective-permute-start.15) | collective-permute-done | bytes 1056 | tf_op jit(solution)/shard_map/ppermute | solution.py:234
  128.8 0.5 slice_bitcast_fusion.2
  129.5 1.3 fusion.1
  (39 shorter events, 1.2 us)
Async XLA Ops:
  2.0 8.8 %collective-permute-start.1 = (bf16[2,128,1024]{2,1,0:T(8,128)(2,1)S(1)}, bf16[2,128,1024]{2,1,0:T(8,128)(2,1)S(1)}, u32[]{:S(2)}, u32[]{:S(2)}) collective-permute-start(bf16[2,128,1024]{2,1,0:T(8,128)(2,1)S(1)} %pad_maximum_fusion.1), channel_id=1, source_target_pairs={{1,0},{2,1},{3,2},{4,3},{5,4},{6,5},{7,6},{8,7},{9,8},{10,9},{11,1... | collective-permute-start | bytes 1572872 | tf_op jit(solution)/shard_map/ppermute | solution.py:248
  10.8 10.7 %collective-permute-start = (bf16[2,128,1024]{2,1,0:T(8,128)(2,1)S(1)}, bf16[2,128,1024]{2,1,0:T(8,128)(2,1)S(1)}, u32[]{:S(2)}, u32[]{:S(2)}) collective-permute-start(bf16[2,128,1024]{2,1,0:T(8,128)(2,1)S(1)} %get-tuple-element.29), channel_id=1, source_target_pairs={{0,1},{1,2},{2,3},{3,4},{4,5},{5,6},{6,7},{7,8},{8,9},{9,10},{10,1... | collective-permute-start | bytes 1572872 | tf_op jit(solution)/shard_map/ppermute | solution.py:247
  16.5 9.7 %collective-permute-start.3 = (bf16[2,128,1024]{2,1,0:T(8,128)(2,1)S(1)}, bf16[2,128,1024]{2,1,0:T(8,128)(2,1)S(1)}, u32[]{:S(2)}, u32[]{:S(2)}) collective-permute-start(bf16[2,128,1024]{2,1,0:T(8,128)(2,1)S(1)} %get-tuple-element.28.hi1_ref), channel_id=1, source_target_pairs={{1,0},{2,1},{3,2},{4,3},{5,4},{6,5},{7,6},{8,7},{9,8},{10,9},{11,1... | collective-permute-start | bytes 1572872 | tf_op jit(solution)/shard_map/ppermute | solution.py:248
  18.5 13.5 %copy-start = (bf16[2,128,1024]{2,1,0:T(8,128)(2,1)S(1)}, bf16[2,128,1024]{2,1,0:T(8,128)(2,1)}, u32[]{:S(2)}) copy-start(bf16[2,128,1024]{2,1,0:T(8,128)(2,1)} %k_ref.1) | copy-start | bytes 1572868
  18.5 13.5 %copy-start.1 = (bf16[2,128,1024]{2,1,0:T(8,128)(2,1)S(1)}, bf16[2,128,1024]{2,1,0:T(8,128)(2,1)}, u32[]{:S(2)}) copy-start(bf16[2,128,1024]{2,1,0:T(8,128)(2,1)} %v_ref.1) | copy-start | bytes 1572868
  18.5 13.5 %copy-start.2 = (bf16[2,128,2048]{2,1,0:T(8,128)(2,1)S(1)}, bf16[2,128,2048]{2,1,0:T(8,128)(2,1)}, u32[]{:S(2)}) copy-start(bf16[2,128,2048]{2,1,0:T(8,128)(2,1)} %q_ref.1) | copy-start | bytes 3145732
  18.5 13.5 %copy-start.3 = (bf16[2,128,2048]{2,1,0:T(8,128)(2,1)S(1)}, bf16[2,128,2048]{2,1,0:T(8,128)(2,1)}, u32[]{:S(2)}) copy-start(bf16[2,128,2048]{2,1,0:T(8,128)(2,1)} %c_ref.1) | copy-start | bytes 3145732
  18.6 13.5 %copy-start.4 = (s32[2,128]{1,0:T(2,128)S(1)}, s32[2,128]{1,0:T(2,128)}, u32[]{:S(2)}) copy-start(s32[2,128]{1,0:T(2,128)} %doc_ref.1) | copy-start | bytes 3076
  18.6 13.5 %copy-start.5 = (f32[128]{0:T(128)S(1)}, f32[128]{0:T(128)}, u32[]{:S(2)}) copy-start(f32[128]{0:T(128)} %param.11) | copy-start | bytes 1540
  18.6 13.5 %copy-start.6 = (f32[128]{0:T(128)S(1)}, f32[128]{0:T(128)}, u32[]{:S(2)}) copy-start(f32[128]{0:T(128)} %param.12) | copy-start | bytes 1540
  21.5 10.5 %collective-permute-start.2 = (bf16[2,128,1024]{2,1,0:T(8,128)(2,1)S(1)}, bf16[2,128,1024]{2,1,0:T(8,128)(2,1)S(1)}, u32[]{:S(2)}, u32[]{:S(2)}) collective-permute-start(bf16[2,128,1024]{2,1,0:T(8,128)(2,1)S(1)} %collective-permute-done.lo1_ref), channel_id=1, source_target_pairs={{0,1},{1,2},{2,3},{3,4},{4,5},{5,6},{6,7},{7,8},{8,9},{9,10},{10,1... | collective-permute-start | bytes 1572872 | tf_op jit(solution)/shard_map/ppermute | solution.py:247
  57.6 8.6 %collective-permute-start.5 = (bf16[2,128,1024]{2,1,0:T(8,128)(2,1)S(1)}, bf16[2,128,1024]{2,1,0:T(8,128)(2,1)S(1)}, u32[]{:S(2)}, u32[]{:S(2)}) collective-permute-start(bf16[2,128,1024]{2,1,0:T(8,128)(2,1)S(1)} %get-tuple-element.20), channel_id=1, source_target_pairs={{1,0},{2,1},{3,2},{4,3},{5,4},{6,5},{7,6},{8,7},{9,8},{10,9},{11,1... | collective-permute-start | bytes 1572872 | tf_op jit(solution)/shard_map/ppermute | solution.py:248
  59.5 11.1 %collective-permute-start.4 = (bf16[2,128,1024]{2,1,0:T(8,128)(2,1)S(1)}, bf16[2,128,1024]{2,1,0:T(8,128)(2,1)S(1)}, u32[]{:S(2)}, u32[]{:S(2)}) collective-permute-start(bf16[2,128,1024]{2,1,0:T(8,128)(2,1)S(1)} %get-tuple-element.18), channel_id=1, source_target_pairs={{0,1},{1,2},{2,3},{3,4},{4,5},{5,6},{6,7},{7,8},{8,9},{9,10},{10,1... | collective-permute-start | bytes 1572872 | tf_op jit(solution)/shard_map/ppermute | solution.py:247
  66.5 11.2 %collective-permute-start.6 = (bf16[2,128,1024]{2,1,0:T(8,128)(2,1)S(1)}, bf16[2,128,1024]{2,1,0:T(8,128)(2,1)S(1)}, u32[]{:S(2)}, u32[]{:S(2)}) collective-permute-start(bf16[2,128,1024]{2,1,0:T(8,128)(2,1)S(1)} %add_convert_fusion), channel_id=1, source_target_pairs={{1,0},{2,1},{3,2},{4,3},{5,4},{6,5},{7,6},{8,7},{9,8},{10,9},{11,1... | collective-permute-start | bytes 1572872 | tf_op jit(solution)/shard_map/ppermute | solution.py:248
  78.0 51.3 %collective-permute-start.7 = (bf16[2,128,1024]{2,1,0:T(8,128)(2,1)S(1)}, bf16[2,128,1024]{2,1,0:T(8,128)(2,1)S(1)}, u32[]{:S(2)}, u32[]{:S(2)}) collective-permute-start(bf16[2,128,1024]{2,1,0:T(8,128)(2,1)S(1)} %get-tuple-element.25), channel_id=1, source_target_pairs={{0,1},{1,2},{2,3},{3,4},{4,5},{5,6},{6,7},{7,8},{8,9},{9,10},{10,1... | collective-permute-start | bytes 1572872 | tf_op jit(solution)/shard_map/ppermute | solution.py:247
  89.3 1.5 %collective-permute-start.8 = (f32[2,128]{1,0:T(2,128)S(1)}, f32[2,128]{1,0:T(2,128)S(1)}, u32[]{:S(2)}, u32[]{:S(2)}) collective-permute-start(f32[2,128]{1,0:T(2,128)S(1)} %get-tuple-element.23), channel_id=1, source_target_pairs={{0,1},{1,0},{2,3},{3,2},{4,5},{5,4},{6,7},{7,6},{8,9},{9,8},{10,11... | collective-permute-start | bytes 3080 | tf_op jit(solution)/shard_map/ppermute | solution.py:234
  90.8 3.6 %collective-permute-start.9 = (f32[2,128]{1,0:T(2,128)S(1)}, f32[2,128]{1,0:T(2,128)S(1)}, u32[]{:S(2)}, u32[]{:S(2)}) collective-permute-start(f32[2,128]{1,0:T(2,128)S(1)} %add.74), channel_id=1, source_target_pairs={{0,2},{1,3},{2,0},{3,1},{4,6},{5,7},{6,4},{7,5},{8,10},{9,11},{10,... | collective-permute-start | bytes 3080 | tf_op jit(solution)/shard_map/ppermute | solution.py:234
  94.4 5.1 %collective-permute-start.10 = (f32[2,128]{1,0:T(2,128)S(1)}, f32[2,128]{1,0:T(2,128)S(1)}, u32[]{:S(2)}, u32[]{:S(2)}) collective-permute-start(f32[2,128]{1,0:T(2,128)S(1)} %add.75), channel_id=1, source_target_pairs={{0,4},{1,5},{2,6},{3,7},{4,0},{5,1},{6,2},{7,3},{8,12},{9,13},{10,... | collective-permute-start | bytes 3080 | tf_op jit(solution)/shard_map/ppermute | solution.py:234
  99.4 3.6 %collective-permute-start.11 = (f32[2,128]{1,0:T(2,128)S(1)}, f32[2,128]{1,0:T(2,128)S(1)}, u32[]{:S(2)}, u32[]{:S(2)}) collective-permute-start(f32[2,128]{1,0:T(2,128)S(1)} %add.76), channel_id=1, source_target_pairs={{0,8},{1,9},{2,10},{3,11},{4,12},{5,13},{6,14},{7,15},{8,0},{9,1},... | collective-permute-start | bytes 3080 | tf_op jit(solution)/shard_map/ppermute | solution.py:234
  103.0 9.7 %collective-permute-start.12 = (f32[2,128]{1,0:T(2,128)S(1)}, f32[2,128]{1,0:T(2,128)S(1)}, u32[]{:S(2)}, u32[]{:S(2)}) collective-permute-start(f32[2,128]{1,0:T(2,128)S(1)} %add.77), channel_id=1, source_target_pairs={{0,16},{1,17},{2,18},{3,19},{4,20},{5,21},{6,22},{7,23},{8,24},{9,... | collective-permute-start | bytes 3080 | tf_op jit(solution)/shard_map/ppermute | solution.py:234
  112.7 7.5 %collective-permute-start.13 = (f32[2,128]{1,0:T(2,128)S(1)}, f32[2,128]{1,0:T(2,128)S(1)}, u32[]{:S(2)}, u32[]{:S(2)}) collective-permute-start(f32[2,128]{1,0:T(2,128)S(1)} %add.78), channel_id=1, source_target_pairs={{0,32},{1,33},{2,34},{3,35},{4,36},{5,37},{6,38},{7,39},{8,40},{9,... | collective-permute-start | bytes 3080 | tf_op jit(solution)/shard_map/ppermute | solution.py:234
  120.2 3.6 %collective-permute-start.14 = (f32[2,128]{1,0:T(2,128)S(1)}, f32[2,128]{1,0:T(2,128)S(1)}, u32[]{:S(2)}, u32[]{:S(2)}) collective-permute-start(f32[2,128]{1,0:T(2,128)S(1)} %add.79), channel_id=1, source_target_pairs={{0,64},{64,0},{128,192},{192,128},{1,65},{65,1},{129,193},{193,129... | collective-permute-start | bytes 3080 | tf_op jit(solution)/shard_map/ppermute | solution.py:234
  123.7 5.1 %collective-permute-start.15 = (f32[2,128]{1,0:T(2,128)S(1)}, f32[2,128]{1,0:T(2,128)S(1)}, u32[]{:S(2)}, u32[]{:S(2)}) collective-permute-start(f32[2,128]{1,0:T(2,128)S(1)} %add.80), channel_id=1, source_target_pairs={{0,128},{64,192},{128,0},{192,64},{1,129},{65,193},{129,1},{193,65... | collective-permute-start | bytes 3080 | tf_op jit(solution)/shard_map/ppermute | solution.py:234

commit v2 on v1

--- a/solution.py
+++ b/solution.py
@@ -32,13 +32,24 @@
     return pltpu.roll(x, x.shape[-1] // 2, 1)
 
 
+def lane_sum(x, terms):
+    width = x.shape[-1]
+    parts = []
+    for _ in range(terms):
+        parts.append(x.astype(BF16))
+        x = x - parts[-1].astype(F32)
+    split = jnp.concatenate(parts, axis=-1)
+    return contract(split, jnp.ones((terms * width, width), BF16), 1, 0)
+
+
 def normalize(x):
-    inverse = lax.rsqrt(jnp.mean(x * x, axis=-1, keepdims=True) + norm_epsilon)
+    inverse = lax.rsqrt(lane_sum(x * x, 2) * (1.0 / x.shape[-1]) + norm_epsilon)
     return x * inverse, inverse
 
 
-def rotate(y, cosine, sine):
-    return y * cosine + half_turn(y) * sine
+def rotate(raw, inverse, gain, cosine, sine):
+    turned = half_turn(raw).astype(F32)
+    return inverse * (raw.astype(F32) * (gain * cosine) + turned * (half_turn(gain) * sine))
 
 
 def unrotate(g, cosine, sine):
@@ -46,7 +57,7 @@
 
 
 def norm_back(grad, normed, inverse):
-    return inverse * (grad - normed * jnp.mean(grad * normed, axis=-1, keepdims=True))
+    return inverse * (grad - normed * (lane_sum(grad * normed, 1) * (1.0 / grad.shape[-1])))
 
 
 def contract(a, b, da, db):
@@ -65,18 +76,18 @@
     k_ref,
     v_ref,
     c_ref,
-    lo1_ref,
-    hi1_ref,
-    lo2_ref,
-    hi2_ref,
+    pair_ref,
+    cross_ref,
+    skip_ref,
+    relay_ref,
     att_ref,
     gq_ref,
     own_k_ref,
     own_v_ref,
-    lo1_out,
-    hi1_out,
-    lo2_out,
-    hi2_out,
+    near_pair_out,
+    near_cross_out,
+    far_pair_out,
+    far_cross_out,
     gains_ref,
     mask_ref,
 ):
@@ -110,12 +121,19 @@
                         x, panel * block : (panel + 1) * block, r * block : (r + 1) * block
                     ] = value
 
-    gain_q = gain_q_ref[...] * query_factor
-    gain_k = gain_k_ref[...]
-    near = (lo1_ref, hi1_ref)
-    far = (lo2_ref, hi2_ref)
-    near_out = (lo1_out, hi1_out)
-    far_out = (lo2_out, hi2_out)
+    gain_q = jnp.broadcast_to(gain_q_ref[...] * query_factor, (block, width))
+    gain_k = jnp.broadcast_to(gain_k_ref[...], (block, width))
+    even = device % 2 == 0
+    at_fold = device == group - 1
+    near, far = [], []
+    for part, own_ref in ((0, k_ref), (1, v_ref)):
+        from_pair, from_cross = pair_ref[part], cross_ref[part]
+        from_skip, from_relay = skip_ref[part], relay_ref[part]
+        high_near = jnp.where(even, from_pair, jnp.where(at_fold, own_ref[0], from_cross))
+        high_far = jnp.where(even, from_relay, jnp.where(at_fold, from_pair, from_skip))
+        near.append((jnp.where(even, from_cross, from_pair), high_near))
+        far.append((jnp.where(even, from_skip, from_relay), high_far))
+    near_grad, far_grad = [], []
     sum_q = jnp.zeros((1, width), F32)
     sum_k = jnp.zeros((1, width), F32)
     for x in range(2):
@@ -126,21 +144,21 @@
             normed, inverse = normalize(q_ref[x, :, r * width : (r + 1) * width].astype(F32))
             q_normed.append(normed)
             q_inverse.append(inverse)
-            q_parts.append(rotate(normed * gain_q, cos_q, sin_q).astype(BF16))
+            q_parts.append(rotate(q_ref[x, :, r * width : (r + 1) * width], inverse, gain_q, cos_q, sin_q).astype(BF16))
             c_parts.append(c_ref[x, :, r * width : (r + 1) * width])
         q_rot = jnp.concatenate(q_parts, axis=0)
         cot = jnp.concatenate(c_parts, axis=0)
-        raw_k = (k_ref[x], near[x][0], far[x][0])
+        raw_k = (k_ref[x], near[0][x], far[0][x])
         k_parts, k_normed, k_inverse = [], [], []
         for panel in range(PANELS):
             normed, inverse = normalize(raw_k[panel].astype(F32))
             k_normed.append(normed)
             k_inverse.append(inverse)
             k_parts.append(
-                rotate(normed * gain_k, cos_ref[x, panel], sin_ref[x, panel]).astype(BF16)
+                rotate(raw_k[panel], inverse, gain_k, cos_ref[x, panel], sin_ref[x, panel]).astype(BF16)
             )
         k_rot = jnp.concatenate(k_parts, axis=0)
-        vals = jnp.concatenate([v_ref[x], near[x][1], far[x][1]], axis=0)
+        vals = jnp.concatenate([v_ref[x], near[1][x], far[1][x]], axis=0)
         expo = jnp.exp(contract(k_rot, q_rot, 1, 1)) * mask_ref[x]
         dprob = contract(vals, cot, 1, 1)
         inverse_total = 1.0 / jnp.sum(expo, axis=0, keepdims=True)
@@ -168,9 +186,16 @@
                 own_k_ref[x] = raw
                 own_v_ref[x] = grad_v[rows]
             else:
-                target = near_out[x] if panel == 1 else far_out[x]
-                target[0] = raw.astype(BF16)
-                target[1] = grad_v[rows].astype(BF16)
+                target = near_grad if panel == 1 else far_grad
+                target.append((raw, grad_v[rows]))
+    for part in range(2):
+        low, high = near_grad[0][part], near_grad[1][part]
+        low_far, high_far = far_grad[0][part], far_grad[1][part]
+        joined = jnp.where(at_fold, low + high_far, low)
+        near_pair_out[part] = jnp.where(even, high, joined).astype(BF16)
+        near_cross_out[part] = jnp.where(even, low, high).astype(BF16)
+        far_pair_out[part] = jnp.where(even, high_far, low_far).astype(BF16)
+        far_cross_out[part] = jnp.where(even, low_far, high_far).astype(BF16)
     gains_ref[0:1, :] += sum_q * query_factor
     gains_ref[1:2, :] += sum_k
 
@@ -227,10 +252,43 @@
     )(device, doc_start, gain_q[None], gain_k[None], cosine, sine, queries, keys, values, cotangent, *panels)
 
 
-def total_over(x, axis):
+def gather_kernel(group, index_ref, own_k_ref, own_v_ref, pair_ref, skip_ref, cross_ref, pay_ref, gk_ref, gv_ref):
+    device = index_ref[0]
+    even = device % 2 == 0
+    at_fold = device == group - 1
+    for part, own_ref, out_ref in ((0, own_k_ref, gk_ref), (1, own_v_ref, gv_ref)):
+        direct = pair_ref[part].astype(F32) + skip_ref[part].astype(F32)
+        across = cross_ref[part].astype(F32) + jnp.where(at_fold, pay_ref[part].astype(F32), 0.0)
+        out_ref[0] = (own_ref[0] + jnp.where(even, direct, across)).astype(BF16)
+        out_ref[1] = (own_ref[1] + jnp.where(even, across, direct)).astype(BF16)
+
+
+def gather(group, device, own_k, own_v, *arrived):
+    _, block, columns = own_k.shape
+    tile = 256
+    spec = pl.BlockSpec((2, block, tile), lambda h: (0, 0, h))
+    return pl.pallas_call(
+        functools.partial(gather_kernel, group),
+        grid=(columns // tile,),
+        in_specs=[pl.BlockSpec(memory_space=pltpu.SMEM)] + [spec] * 6,
+        out_specs=[spec, spec],
+        out_shape=[jax.ShapeDtypeStruct(own_k.shape, BF16)] * 2,
+        compiler_params=pltpu.CompilerParams(dimension_semantics=("arbitrary",)),
+        cost_estimate=pl.CostEstimate(
+            flops=8 * own_k.size, bytes_accessed=16 * own_k.size, transcendentals=0
+        ),
+        name="gather",
+    )(device, own_k, own_v, *arrived)
+
+
+def move(x, pairs):
+    return lax.ppermute(x, "ctx", pairs)
+
+
+def total_over(x, axis, first, last):
     size = lax.axis_size(axis)
-    distance = 1
-    while distance < size:
+    distance = first
+    while distance < last:
         x = x + lax.ppermute(x, axis, [(i, i ^ distance) for i in range(size)])
         distance *= 2
     return x
@@ -241,19 +299,25 @@
     block = queries.shape[1]
     width = gain_q.shape[0]
     device = lax.axis_index("ctx")
+    index = device[None].astype(jnp.int32)
+    even = device % 2 == 0
     at_fold = device == group - 1
-    upward = [(i, i + 1) for i in range(group - 1)]
-    downward = [(i + 1, i) for i in range(group - 1)]
-    up = lambda a: lax.ppermute(a, "ctx", upward)
-    down = lambda a: lax.ppermute(a, "ctx", downward)
+    evens = range(0, group, 2)
+    pairs = [(i, i ^ 1) for i in range(group)]
+    cross = [(i + 1, i + 2) for i in evens if i + 2 < group]
+    cross = cross + [(b, a) for a, b in cross]
+    skip_in = [(i, i + 2) for i in evens if i + 2 < group]
+    skip_in = skip_in + [(i + 3, i + 1) for i in evens if i + 3 < group]
+    skip_out = [(b, a) for a, b in skip_in]
 
     low = jnp.stack([keys[0], values[0]])
     high = jnp.stack([keys[1], values[1]])
-    low1 = up(low)
-    high1 = jnp.where(at_fold, low, down(high))
-    low2 = up(low1)
-    high2 = down(high1)
-    high2 = jnp.where(at_fold, low1, high2)
+    first = jnp.where(even, low, high)
+    second = jnp.where(even, high, low)
+    from_cross = move(second, cross)
+    from_skip = move(first, skip_in)
+    from_pair = move(first, pairs)
+    from_relay = move(jnp.where(at_fold, second, from_cross), pairs)
 
     rows = jnp.arange(block, dtype=jnp.int32)
     slots = jnp.stack([device, 2 * group - 1 - device])[:, None] - jnp.arange(PANELS)[None, :]
@@ -263,9 +327,9 @@
     cosine = jnp.concatenate([cosine, cosine], axis=-1)
     sine = jnp.concatenate([-sine, sine], axis=-1)
 
-    attended, grad_queries, own_k, own_v, low1_g, high1_g, low2_g, high2_g, gains = attend(
+    attended, grad_queries, own_k, own_v, near_pair, near_cross, far_pair, far_cross, gains = attend(
         group,
-        device[None].astype(jnp.int32),
+        index,
         doc_start,
         gain_q,
         key_norm_gain,
@@ -275,18 +339,17 @@
         keys,
         values,
         cotangent,
-        (low1, high1, low2, high2),
+        (from_pair, from_cross, from_skip, from_relay),
     )
-    back_low = jnp.where(at_fold, high2_g, down(low2_g))
-    back_high = up(high2_g)
-    back_low = (back_low.astype(F32) + low1_g.astype(F32)).astype(BF16)
-    back_high = (back_high.astype(F32) + high1_g.astype(F32)).astype(BF16)
-    home_low = jnp.where(at_fold, back_high, down(back_low))
-    home_high = up(back_high)
-    gains = total_over(total_over(gains, "ctx"), "dp")
-    home = jnp.stack([home_low, home_high], axis=1).astype(F32)
-    grad_keys = (own_k + home[0]).astype(BF16)
-    grad_values = (own_v + home[1]).astype(BF16)
+    back_relay = move(far_pair, pairs)
+    back_pair = move(near_pair, pairs)
+    back_skip = move(far_cross, skip_out)
+    pay = (near_cross.astype(F32) + back_relay.astype(F32)).astype(BF16)
+    back_cross = move(pay, cross)
+    everyone = lax.axis_size("ctx") * lax.axis_size("dp")
+    spread = jnp.broadcast_to(gains[None], (everyone,) + gains.shape)
+    gains = jnp.sum(lax.all_to_all(spread, ("dp", "ctx"), 0, 0, tiled=True), axis=0)
+    grad_keys, grad_values = gather(group, index, own_k, own_v, back_pair, back_skip, back_cross, pay)
     return attended, grad_queries, grad_keys, grad_values, gains[0], gains[1]
 
 

time: 131 us -> 86.3 us (0.66)
  the two profiles are of different devices: /device:TPU:62 before, /device:TPU:1 now
where the time goes in v2:
time: 86.3 us; the launch traced here: 85.9 us
  starting transfers between devices  32.6 us (38%)
  Pallas kernels  24.1 us (28%)
  waiting for transfers between devices  17.7 us (21%)
  local copies, waits for them, and re-layouts  6.96 us (8%)
  other arithmetic  3.69 us (4%)
    pallas_call x1, Pallas kernels, attend(): pl.pallas_call(functools.partial(attend_kernel, group), grid=(heads,), in...  20.1 us
    ppermute x8, starting transfers between devices, move(): return lax.ppermute(x, 'ctx', pairs)  16.5 us
    all_to_all x1, starting transfers between devices, shards(): lax.all_to_all(spread, ('dp', 'ctx'), 0, 0, tiled=True)  16.1 us
    ppermute x8, waiting for transfers between devices, move(): return lax.ppermute(x, 'ctx', pairs)  11.8 us
    all_to_all x1, waiting for transfers between devices, shards(): lax.all_to_all(spread, ('dp', 'ctx'), 0, 0, tiled=True)  5.88 us
    unnamed x26, local copies, waits for them, and re-layouts  4.41 us
    pallas_call x1, Pallas kernels, gather(): pl.pallas_call(functools.partial(gather_kernel, group), grid=(columns //...  4 us
  transfers between devices with their start and end apart: 9, of which 3 were waited for; matrix products, arithmetic and copies ran while one was open for 6% of the time, Pallas kernels for 0%

profile of v2, /device:TPU:1, one launch (start us, length us, event | category | flops | bytes accessed | tf_op | source)
XLA Modules:
  0.0 85.9 jit_solution(9924891026612333168)
XLA Ops:
  0.6 1.3 %fusion.3 = (bf16[1,128,1024]{2,1,0:T(8,128)(2,1)S(1)}, bf16[1,128,1024]{2,1,0:T(8,128)(2,1)S(1)}, bf16[1,128,1024]{2,1,0:T(8,128)(2,1)S(1)}, bf16[1,128,1024]{2,1,0:T(8,128)(2,1)S(1)}) fusion(bf16[2,128,1024]{2,1,0:T(8,128)(2,1)} %k_ref.1, bf16[2,128,1024]{2,1,0:T(8,128)(2,1)} %v_ref.1), kind=kLoop, calls=%fused_computation.21 | loop fusion | bytes 2097152 | tf_op jit(solution)/shard_map/slice | solution.py:313
  1.9 0.1 broadcast_select_fusion.1
  2.0 1.3 %collective-permute-start.2 = (bf16[2,128,1024]{2,1,0:T(8,128)(2,1)S(1)}, bf16[2,128,1024]{2,1,0:T(8,128)(2,1)S(1)}, u32[]{:S(2)}, u32[]{:S(2)}) collective-permute-start(bf16[2,128,1024]{2,1,0:T(8,128)(2,1)S(1)} %get-tuple-element.29), channel_id=1, source_target_pairs={{0,2},{2,4},{4,6},{6,8},{8,10},{10,12},{12,14},{14,16},{16,18},{18... | collective-permute-start | bytes 1572872 | tf_op jit(solution)/shard_map/ppermute | solution.py:285
  3.3 3.8 %collective-permute-start = (bf16[2,128,1024]{2,1,0:T(8,128)(2,1)S(1)}, bf16[2,128,1024]{2,1,0:T(8,128)(2,1)S(1)}, u32[]{:S(2)}, u32[]{:S(2)}) collective-permute-start(bf16[2,128,1024]{2,1,0:T(8,128)(2,1)S(1)} %get-tuple-element.29), channel_id=1, source_target_pairs={{0,1},{1,0},{2,3},{3,2},{4,5},{5,4},{6,7},{7,6},{8,9},{9,8},{10,11... | collective-permute-start | bytes 1572872 | tf_op jit(solution)/shard_map/ppermute | solution.py:285
  7.1 3.1 %collective-permute-start.1 = (bf16[2,128,1024]{2,1,0:T(8,128)(2,1)S(1)}, bf16[2,128,1024]{2,1,0:T(8,128)(2,1)S(1)}, u32[]{:S(2)}, u32[]{:S(2)}) collective-permute-start(bf16[2,128,1024]{2,1,0:T(8,128)(2,1)S(1)} %get-tuple-element.28), channel_id=1, source_target_pairs={{1,2},{3,4},{5,6},{7,8},{9,10},{11,12},{13,14},{15,16},{17,18},{19... | collective-permute-start | bytes 1572872 | tf_op jit(solution)/shard_map/ppermute | solution.py:285
  10.2 0.1 pad_add_fusion
  10.3 0.1 compare_and_fusion
  10.4 0.1 fusion.2
  10.4 8.5 %collective-permute-done.1.cross_ref = bf16[2,128,1024]{2,1,0:T(8,128)(2,1)S(1)} collective-permute-done((bf16[2,128,1024]{2,1,0:T(8,128)(2,1)S(1)}, bf16[2,128,1024]{2,1,0:T(8,128)(2,1)S(1)}, u32[]{:S(2)}, u32[]{:S(2)}) %collective-permute-start.1) | collective-permute-done | bytes 524320 | tf_op jit(solution)/shard_map/ppermute | solution.py:285
  19.0 0.1 collective-permute-start.3
  19.1 0.1 select_convert_fusion
  19.2 1.4 %fusion = (f32[2,3,128,64]{3,2,1,0:T(8,128)S(1)}, f32[2,3,128,64]{3,2,1,0:T(8,128)S(1)}, f32[2,3,128,64]{3,2,1,0:T(8,128)S(1)}) fusion(f32[64]{0:T(128)S(1)} %multiply_exponential_fusion, f32[2,3,128]{2,1,0:T(4,128)S(1)} %select_convert_fusion), kind=kLoop, calls=%fused_computation.10 | loop fusion | flops 98304 | bytes 593152 | tf_op jit(solution)/shard_map/neg | solution.py:328
  20.7 0.3 pad_maximum_fusion.2
  21.0 0.7 copy-done.2
  21.7 0.2 copy-done.3
  21.9 20.1 %attend.1 = (bf16[2,128,2048]{2,1,0:T(8,128)(2,1)}, bf16[2,128,2048]{2,1,0:T(8,128)(2,1)}, f32[2,128,1024]{2,1,0:T(8,128)S(1)}, f32[2,128,1024]{2,1,0:T(8,128)S(...) custom-call(s32[1]{0:T(128)} %bitcast.index_ref, ...), custom_call_target="tpu_custom_call" | custom-call | flops 2415919104 | bytes 12582912 | tf_op jit(solution)/shard_map/attend/pallas_call | solution.py:213
  42.0 1.0 %copy-done = f32[2,128,1024]{2,1,0:T(8,128)} copy-done((f32[2,128,1024]{2,1,0:T(8,128)}, f32[2,128,1024]{2,1,0:T(8,128)S(1)}, u32[]{:S(2)}) %copy-start) | copy-done | bytes 1048600
  42.9 1.0 %copy-done.1 = f32[2,128,1024]{2,1,0:T(8,128)} copy-done((f32[2,128,1024]{2,1,0:T(8,128)}, f32[2,128,1024]{2,1,0:T(8,128)S(1)}, u32[]{:S(2)}) %copy-start.1) | copy-done | bytes 1048600
  43.9 0.5 collective-permute-start.6
  44.4 0.8 broadcast_in_dim.48
  45.2 16.1 %all-to-all-start = ((f32[256,2,128]{2,1,0:T(2,128)}), f32[256,2,128]{2,1,0:T(2,128)S(1)}, u32[]{:S(2)}, u32[]{:S(2)}) async-start(f32[256,2,128]{2,1,0:T(2,128)} %broadcast_in_dim.48), calls=%async_computation | async-start | bytes 524288 | tf_op jit(solution)/shard_map/all_to_all | solution.py:351
  61.3 2.2 %collective-permute-start.4 = (bf16[2,128,1024]{2,1,0:T(8,128)(2,1)S(1)}, bf16[2,128,1024]{2,1,0:T(8,128)(2,1)S(1)}, u32[]{:S(2)}, u32[]{:S(2)}) collective-permute-start(bf16[2,128,1024]{2,1,0:T(8,128)(2,1)S(1)} %get-tuple-element.21), channel_id=1, source_target_pairs={{0,1},{1,0},{2,3},{3,2},{4,5},{5,4},{6,7},{7,6},{8,9},{9,8},{10,11... | collective-permute-start | bytes 1572872 | tf_op jit(solution)/shard_map/ppermute | solution.py:285
  63.5 2.3 %collective-permute-start.5 = (bf16[2,128,1024]{2,1,0:T(8,128)(2,1)S(1)}, bf16[2,128,1024]{2,1,0:T(8,128)(2,1)}, u32[]{:S(2)}, u32[]{:S(2)}) collective-permute-start(bf16[2,128,1024]{2,1,0:T(8,128)(2,1)S(1)} %get-tuple-element.22), channel_id=1, source_target_pairs={{2,0},{4,2},{6,4},{8,6},{10,8},{12,10},{14,12},{16,14},{18,16},{20... | collective-permute-start | bytes 1572872 | tf_op jit(solution)/shard_map/ppermute | solution.py:285
  65.8 0.8 copy-done.12
  66.6 1.2 %add_convert_fusion.pay_ref = bf16[2,128,1024]{2,1,0:T(8,128)(2,1)S(1)} fusion(bf16[2,128,1024]{2,1,0:T(8,128)(2,1)} %copy-done.12, bf16[2,128,1024]{2,1,0:T(8,128)(2,1)S(1)} %get-tuple-element.23), kind=kLoop, calls=%fused_computation | loop fusion | flops 1048576 | bytes 1572864 | tf_op jit(solution)/shard_map/convert_element_type | solution.py:347
  67.9 3.2 %collective-permute-start.7 = (bf16[2,128,1024]{2,1,0:T(8,128)(2,1)S(1)}, bf16[2,128,1024]{2,1,0:T(8,128)(2,1)S(1)}, u32[]{:S(2)}, u32[]{:S(2)}) collective-permute-start(bf16[2,128,1024]{2,1,0:T(8,128)(2,1)S(1)} %add_convert_fusion.pay_ref), channel_id=1, source_target_pairs={{1,2},{3,4},{5,6},{7,8},{9,10},{11,12},{13,14},{15,16},{17,18},{19... | collective-permute-start | bytes 1572872 | tf_op jit(solution)/shard_map/ppermute | solution.py:285
  71.1 5.9 %all-to-all-done = f32[256,2,128]{2,1,0:T(2,128)S(1)} async-done(((f32[256,2,128]{2,1,0:T(2,128)}), f32[256,2,128]{2,1,0:T(2,128)S(1)}, u32[]{:S(2)}, u32[]{:S(2)}) %all-to-all-start) | async-done | bytes 262176 | tf_op jit(solution)/shard_map/all_to_all | solution.py:351
  77.0 0.3 reduce_sum.9
  77.2 0.5 slice_bitcast_fusion
  77.8 3.3 %collective-permute-done.7.cross_ref = bf16[2,128,1024]{2,1,0:T(8,128)(2,1)S(1)} collective-permute-done((bf16[2,128,1024]{2,1,0:T(8,128)(2,1)S(1)}, bf16[2,128,1024]{2,1,0:T(8,128)(2,1)S(1)}, u32[]{:S(2)}, u32[]{:S(2)}) %collective-permute-start.7) | collective-permute-done | bytes 524320 | tf_op jit(solution)/shard_map/ppermute | solution.py:285
  81.1 0.8 copy-done.11
  81.9 4.0 %gather.1 = (bf16[2,128,1024]{2,1,0:T(8,128)(2,1)}, bf16[2,128,1024]{2,1,0:T(8,128)(2,1)}) custom-call(s32[1]{0:T(128)} %bitcast.index_ref, f32[2,128,1024]{2,1,0:T(8,128)} %copy-done, f32[2,128,1024]{2,1,0:T(8,128)} %copy-done.1, bf16[2,128,1024]{2,1,0:T(8,128)(2,1)} %copy-done.10, bf16[2,128,1024]{2,1,0:T(8,128)(2,1)} %collective-permute-done.5.skip_ref, ...), custom_call_target="tpu_custom_call" | custom-call | flops 2097152 | bytes 4194304 | tf_op jit(solution)/shard_map/gather/pallas_call | solution.py:270
  (28 shorter events, 0.1 us)
Async XLA Ops:
  2.0 18.9 %collective-permute-start.2 = (bf16[2,128,1024]{2,1,0:T(8,128)(2,1)S(1)}, bf16[2,128,1024]{2,1,0:T(8,128)(2,1)S(1)}, u32[]{:S(2)}, u32[]{:S(2)}) collective-permute-start(bf16[2,128,1024]{2,1,0:T(8,128)(2,1)S(1)} %get-tuple-element.29), channel_id=1, source_target_pairs={{0,2},{2,4},{4,6},{6,8},{8,10},{10,12},{12,14},{14,16},{16,18},{18... | collective-permute-start | bytes 1572872 | tf_op jit(solution)/shard_map/ppermute | solution.py:285
  3.3 17.6 %collective-permute-start = (bf16[2,128,1024]{2,1,0:T(8,128)(2,1)S(1)}, bf16[2,128,1024]{2,1,0:T(8,128)(2,1)S(1)}, u32[]{:S(2)}, u32[]{:S(2)}) collective-permute-start(bf16[2,128,1024]{2,1,0:T(8,128)(2,1)S(1)} %get-tuple-element.29), channel_id=1, source_target_pairs={{0,1},{1,0},{2,3},{3,2},{4,5},{5,4},{6,7},{7,6},{8,9},{9,8},{10,11... | collective-permute-start | bytes 1572872 | tf_op jit(solution)/shard_map/ppermute | solution.py:285
  7.1 11.8 %collective-permute-start.1 = (bf16[2,128,1024]{2,1,0:T(8,128)(2,1)S(1)}, bf16[2,128,1024]{2,1,0:T(8,128)(2,1)S(1)}, u32[]{:S(2)}, u32[]{:S(2)}) collective-permute-start(bf16[2,128,1024]{2,1,0:T(8,128)(2,1)S(1)} %get-tuple-element.28), channel_id=1, source_target_pairs={{1,2},{3,4},{5,6},{7,8},{9,10},{11,12},{13,14},{15,16},{17,18},{19... | collective-permute-start | bytes 1572872 | tf_op jit(solution)/shard_map/ppermute | solution.py:285
  19.0 2.0 %collective-permute-start.3 = (bf16[2,128,1024]{2,1,0:T(8,128)(2,1)S(1)}, bf16[2,128,1024]{2,1,0:T(8,128)(2,1)S(1)}, u32[]{:S(2)}, u32[]{:S(2)}) collective-permute-start(bf16[2,128,1024]{2,1,0:T(8,128)(2,1)S(1)} %broadcast_select_fusion), channel_id=1, source_target_pairs={{0,1},{1,0},{2,3},{3,2},{4,5},{5,4},{6,7},{7,6},{8,9},{9,8},{10,11... | collective-permute-start | bytes 1572872 | tf_op jit(solution)/shard_map/ppermute | solution.py:285
  19.2 1.8 %copy-start.4 = (bf16[2,128,2048]{2,1,0:T(8,128)(2,1)S(1)}, bf16[2,128,2048]{2,1,0:T(8,128)(2,1)}, u32[]{:S(2)}) copy-start(bf16[2,128,2048]{2,1,0:T(8,128)(2,1)} %q_ref.1) | copy-start | bytes 3145732
  19.2 1.8 %copy-start.5 = (bf16[2,128,2048]{2,1,0:T(8,128)(2,1)S(1)}, bf16[2,128,2048]{2,1,0:T(8,128)(2,1)}, u32[]{:S(2)}) copy-start(bf16[2,128,2048]{2,1,0:T(8,128)(2,1)} %c_ref.1) | copy-start | bytes 3145732
  20.6 1.1 %copy-start.2 = (bf16[2,128,1024]{2,1,0:T(8,128)(2,1)S(1)}, bf16[2,128,1024]{2,1,0:T(8,128)(2,1)}, u32[]{:S(2)}) copy-start(bf16[2,128,1024]{2,1,0:T(8,128)(2,1)} %k_ref.1) | copy-start | bytes 1572868
  20.6 1.2 %copy-start.3 = (bf16[2,128,1024]{2,1,0:T(8,128)(2,1)S(1)}, bf16[2,128,1024]{2,1,0:T(8,128)(2,1)}, u32[]{:S(2)}) copy-start(bf16[2,128,1024]{2,1,0:T(8,128)(2,1)} %v_ref.1) | copy-start | bytes 1572868
  20.7 1.2 %copy-start.8 = (f32[128]{0:T(128)S(1)}, f32[128]{0:T(128)}, u32[]{:S(2)}) copy-start(f32[128]{0:T(128)} %param.12) | copy-start | bytes 1540
  21.0 0.9 %copy-start.6 = (s32[2,128]{1,0:T(2,128)S(1)}, s32[2,128]{1,0:T(2,128)}, u32[]{:S(2)}) copy-start(s32[2,128]{1,0:T(2,128)} %doc_ref.1) | copy-start | bytes 3076
  21.0 0.9 %copy-start.7 = (f32[128]{0:T(128)S(1)}, f32[128]{0:T(128)}, u32[]{:S(2)}) copy-start(f32[128]{0:T(128)} %param.11) | copy-start | bytes 1540
  42.0 1.0 %copy-start = (f32[2,128,1024]{2,1,0:T(8,128)}, f32[2,128,1024]{2,1,0:T(8,128)S(1)}, u32[]{:S(2)}) copy-start(f32[2,128,1024]{2,1,0:T(8,128)S(1)} %get-tuple-element.19.own_k_ref) | copy-start | bytes 3145732
  42.9 1.0 %copy-start.1 = (f32[2,128,1024]{2,1,0:T(8,128)}, f32[2,128,1024]{2,1,0:T(8,128)S(1)}, u32[]{:S(2)}) copy-start(f32[2,128,1024]{2,1,0:T(8,128)S(1)} %get-tuple-element.20.own_v_ref) | copy-start | bytes 3145732
  43.9 21.9 %collective-permute-start.6 = (bf16[2,128,1024]{2,1,0:T(8,128)(2,1)}, bf16[2,128,1024]{2,1,0:T(8,128)(2,1)S(1)}, u32[]{:S(2)}, u32[]{:S(2)}) collective-permute-start(bf16[2,128,1024]{2,1,0:T(8,128)(2,1)} %get-tuple-element.24), channel_id=1, source_target_pairs={{0,1},{1,0},{2,3},{3,2},{4,5},{5,4},{6,7},{7,6},{8,9},{9,8},{10,11... | collective-permute-start | bytes 1572872 | tf_op jit(solution)/shard_map/ppermute | solution.py:285
  45.2 31.8 %all-to-all-start = ((f32[256,2,128]{2,1,0:T(2,128)}), f32[256,2,128]{2,1,0:T(2,128)S(1)}, u32[]{:S(2)}, u32[]{:S(2)}) async-start(f32[256,2,128]{2,1,0:T(2,128)} %broadcast_in_dim.48), calls=%async_computation | async-start | bytes 524288 | tf_op jit(solution)/shard_map/all_to_all | solution.py:351
  61.3 16.5 %collective-permute-start.4 = (bf16[2,128,1024]{2,1,0:T(8,128)(2,1)S(1)}, bf16[2,128,1024]{2,1,0:T(8,128)(2,1)S(1)}, u32[]{:S(2)}, u32[]{:S(2)}) collective-permute-start(bf16[2,128,1024]{2,1,0:T(8,128)(2,1)S(1)} %get-tuple-element.21), channel_id=1, source_target_pairs={{0,1},{1,0},{2,3},{3,2},{4,5},{5,4},{6,7},{7,6},{8,9},{9,8},{10,11... | collective-permute-start | bytes 1572872 | tf_op jit(solution)/shard_map/ppermute | solution.py:285
  63.5 14.2 %collective-permute-start.5 = (bf16[2,128,1024]{2,1,0:T(8,128)(2,1)S(1)}, bf16[2,128,1024]{2,1,0:T(8,128)(2,1)}, u32[]{:S(2)}, u32[]{:S(2)}) collective-permute-start(bf16[2,128,1024]{2,1,0:T(8,128)(2,1)S(1)} %get-tuple-element.22), channel_id=1, source_target_pairs={{2,0},{4,2},{6,4},{8,6},{10,8},{12,10},{14,12},{16,14},{18,16},{20... | collective-permute-start | bytes 1572872 | tf_op jit(solution)/shard_map/ppermute | solution.py:285
  65.8 0.8 copy-start.12
  67.9 13.2 %copy-start.9 = (bf16[2,128,1024]{2,1,0:T(8,128)(2,1)}, bf16[2,128,1024]{2,1,0:T(8,128)(2,1)S(1)}, u32[]{:S(2)}) copy-start(bf16[2,128,1024]{2,1,0:T(8,128)(2,1)S(1)} %add_convert_fusion.pay_ref) | copy-start | bytes 1572868
  67.9 13.2 %collective-permute-start.7 = (bf16[2,128,1024]{2,1,0:T(8,128)(2,1)S(1)}, bf16[2,128,1024]{2,1,0:T(8,128)(2,1)S(1)}, u32[]{:S(2)}, u32[]{:S(2)}) collective-permute-start(bf16[2,128,1024]{2,1,0:T(8,128)(2,1)S(1)} %add_convert_fusion.pay_ref), channel_id=1, source_target_pairs={{1,2},{3,4},{5,6},{7,8},{9,10},{11,12},{13,14},{15,16},{17,18},{19... | collective-permute-start | bytes 1572872 | tf_op jit(solution)/shard_map/ppermute | solution.py:285
  77.8 3.3 %copy-start.10 = (bf16[2,128,1024]{2,1,0:T(8,128)(2,1)}, bf16[2,128,1024]{2,1,0:T(8,128)(2,1)S(1)}, u32[]{:S(2)}) copy-start(bf16[2,128,1024]{2,1,0:T(8,128)(2,1)S(1)} %collective-permute-done.4.pair_ref) | copy-start | bytes 1572868
  81.1 0.8 copy-start.11

commit v3 on v2

--- a/solution.py
+++ b/solution.py
@@ -62,6 +62,59 @@
 
 def contract(a, b, da, db):
     return lax.dot_general(a, b, (((da,), (db,)), ((), ())), preferred_element_type=F32)
+
+
+def in_hbm(x):
+    return pltpu.with_memory_space_constraint(x, pltpu.HBM)
+
+
+def prepare_kernel(gain_q_ref, gain_k_ref, cos_ref, sin_ref, q_ref, k_ref, qr_ref, qi_ref, kr_ref, ki_ref):
+    width = gain_q_ref.shape[1]
+    jobs = []
+    for x in range(2):
+        jobs.append((x, k_ref, kr_ref, ki_ref, slice(0, width), gain_k_ref[...]))
+        for r in range(q_ref.shape[2] // width):
+            cols = slice(r * width, (r + 1) * width)
+            jobs.append((x, q_ref, qr_ref, qi_ref, cols, gain_q_ref[...] * query_factor))
+    norms = [normalize(src[x, :, cols].astype(F32))[1] for x, src, _, _, cols, _ in jobs]
+    for inverse, (x, src, out, inv_out, cols, gain) in zip(norms, jobs):
+        gain = jnp.broadcast_to(gain, inverse.shape)
+        turned = rotate(src[x, :, cols], inverse, gain, cos_ref[x], sin_ref[x])
+        out[x, :, cols] = turned.astype(BF16)
+        inv_out[x, :, cols] = inverse
+
+
+def prepare(gain_q, gain_k, cosine, sine, queries, keys):
+    _, block, columns = keys.shape
+    width = gain_q.shape[0]
+    repeat = queries.shape[2] // columns
+    whole = lambda shape: pl.BlockSpec(shape, lambda h: (0,) * len(shape))
+    wide = pl.BlockSpec((2, block, repeat * width), lambda h: (0, 0, h))
+    slim = pl.BlockSpec((2, block, width), lambda h: (0, 0, h))
+    return pl.pallas_call(
+        prepare_kernel,
+        grid=(columns // width,),
+        in_specs=[
+            whole((1, width)),
+            whole((1, width)),
+            whole((2, block, width)),
+            whole((2, block, width)),
+            wide,
+            slim,
+        ],
+        out_specs=[wide, wide, slim, slim],
+        out_shape=[
+            pltpu.HBM(queries.shape, BF16),
+            pltpu.HBM(queries.shape, F32),
+            pltpu.HBM(keys.shape, BF16),
+            pltpu.HBM(keys.shape, F32),
+        ],
+        compiler_params=pltpu.CompilerParams(dimension_semantics=("arbitrary",)),
+        cost_estimate=pl.CostEstimate(
+            flops=64 * queries.size, bytes_accessed=16 * queries.size, transcendentals=queries.size
+        ),
+        name="prepare",
+    )(gain_q[None], gain_k[None], cosine, sine, in_hbm(queries), in_hbm(keys))
 
 
 def attend_kernel(
@@ -80,6 +133,10 @@
     cross_ref,
     skip_ref,
     relay_ref,
+    qr_ref,
+    qi_ref,
+    kr_ref,
+    ki_ref,
     att_ref,
     gq_ref,
     own_k_ref,
@@ -134,60 +191,67 @@
         near.append((jnp.where(even, from_cross, from_pair), high_near))
         far.append((jnp.where(even, from_skip, from_relay), high_far))
     near_grad, far_grad = [], []
+    halves = range(2)
+    sides = range(repeat)
+    spans = range(PANELS)
+    cols = [slice(r * width, (r + 1) * width) for r in sides]
+    raw_q = [[q_ref[x, :, cols[r]] for r in sides] for x in halves]
+    raw_k = [(k_ref[x], near[0][x], far[0][x]) for x in halves]
+    k_norm = [
+        [(raw_k[x][0].astype(F32) * ki_ref[x], ki_ref[x])]
+        + [normalize(raw_k[x][p].astype(F32)) for p in spans[1:]]
+        for x in halves
+    ]
+    q_rot = [jnp.concatenate([qr_ref[x, :, cols[r]] for r in sides], axis=0) for x in halves]
+    k_rot = [
+        jnp.concatenate(
+            [kr_ref[x]]
+            + [
+                rotate(raw_k[x][p], k_norm[x][p][1], gain_k, cos_ref[x, p], sin_ref[x, p]).astype(BF16)
+                for p in spans[1:]
+            ],
+            axis=0,
+        )
+        for x in halves
+    ]
+    cot = [jnp.concatenate([c_ref[x, :, cols[r]] for r in sides], axis=0) for x in halves]
+    vals = [jnp.concatenate([v_ref[x], near[1][x], far[1][x]], axis=0) for x in halves]
+    score = [contract(k_rot[x], q_rot[x], 1, 1) for x in halves]
+    dprob = [contract(vals[x], cot[x], 1, 1) for x in halves]
+    probs, dscore = [], []
+    for x in halves:
+        expo = jnp.exp(score[x]) * mask_ref[x]
+        prob = expo * (1.0 / jnp.sum(expo, axis=0, keepdims=True))
+        delta = jnp.sum(prob * dprob[x], axis=0, keepdims=True)
+        dscore.append((prob * (dprob[x] - delta)).astype(BF16))
+        probs.append(prob.astype(BF16))
+    grad_v = [contract(probs[x], cot[x], 1, 0) for x in halves]
+    grad_k = [contract(dscore[x], q_rot[x], 1, 0) for x in halves]
+    grad_q = [contract(dscore[x], k_rot[x], 0, 0) for x in halves]
+    attended = [contract(probs[x], vals[x], 0, 0) for x in halves]
     sum_q = jnp.zeros((1, width), F32)
     sum_k = jnp.zeros((1, width), F32)
-    for x in range(2):
-        cos_q = cos_ref[x, 0]
-        sin_q = sin_ref[x, 0]
-        q_parts, q_normed, q_inverse, c_parts = [], [], [], []
-        for r in range(repeat):
-            normed, inverse = normalize(q_ref[x, :, r * width : (r + 1) * width].astype(F32))
-            q_normed.append(normed)
-            q_inverse.append(inverse)
-            q_parts.append(rotate(q_ref[x, :, r * width : (r + 1) * width], inverse, gain_q, cos_q, sin_q).astype(BF16))
-            c_parts.append(c_ref[x, :, r * width : (r + 1) * width])
-        q_rot = jnp.concatenate(q_parts, axis=0)
-        cot = jnp.concatenate(c_parts, axis=0)
-        raw_k = (k_ref[x], near[0][x], far[0][x])
-        k_parts, k_normed, k_inverse = [], [], []
-        for panel in range(PANELS):
-            normed, inverse = normalize(raw_k[panel].astype(F32))
-            k_normed.append(normed)
-            k_inverse.append(inverse)
-            k_parts.append(
-                rotate(raw_k[panel], inverse, gain_k, cos_ref[x, panel], sin_ref[x, panel]).astype(BF16)
-            )
-        k_rot = jnp.concatenate(k_parts, axis=0)
-        vals = jnp.concatenate([v_ref[x], near[1][x], far[1][x]], axis=0)
-        expo = jnp.exp(contract(k_rot, q_rot, 1, 1)) * mask_ref[x]
-        dprob = contract(vals, cot, 1, 1)
-        inverse_total = 1.0 / jnp.sum(expo, axis=0, keepdims=True)
-        probs = expo * inverse_total
-        delta = jnp.sum(probs * dprob, axis=0, keepdims=True)
-        dscore = (probs * (dprob - delta)).astype(BF16)
-        probs = probs.astype(BF16)
-        attended = contract(probs, vals, 0, 0)
-        grad_q = contract(dscore, k_rot, 0, 0)
-        grad_v = contract(probs, cot, 1, 0)
-        grad_k = contract(dscore, q_rot, 1, 0)
-        for r in range(repeat):
+    for x in halves:
+        for p in spans:
+            rows = slice(p * block, (p + 1) * block)
+            normed, inverse = k_norm[x][p]
+            back = unrotate(grad_k[x][rows], cos_ref[x, p], sin_ref[x, p])
+            sum_k = sum_k + jnp.sum(back * normed, axis=0, keepdims=True)
+            raw = norm_back(back * gain_k, normed, inverse)
+            if p == 0:
+                own_k_ref[x] = raw
+                own_v_ref[x] = grad_v[x][rows]
+            else:
+                target = near_grad if p == 1 else far_grad
+                target.append((raw, grad_v[x][rows]))
+        for r in sides:
             rows = slice(r * block, (r + 1) * block)
-            cols = slice(r * width, (r + 1) * width)
-            att_ref[x, :, cols] = attended[rows].astype(BF16)
-            back = unrotate(grad_q[rows], cos_q, sin_q)
-            sum_q = sum_q + jnp.sum(back * q_normed[r], axis=0, keepdims=True)
-            gq_ref[x, :, cols] = norm_back(back * gain_q, q_normed[r], q_inverse[r]).astype(BF16)
-        for panel in range(PANELS):
-            rows = slice(panel * block, (panel + 1) * block)
-            back = unrotate(grad_k[rows], cos_ref[x, panel], sin_ref[x, panel])
-            sum_k = sum_k + jnp.sum(back * k_normed[panel], axis=0, keepdims=True)
-            raw = norm_back(back * gain_k, k_normed[panel], k_inverse[panel])
-            if panel == 0:
-                own_k_ref[x] = raw
-                own_v_ref[x] = grad_v[rows]
-            else:
-                target = near_grad if panel == 1 else far_grad
-                target.append((raw, grad_v[rows]))
+            inverse = qi_ref[x, :, cols[r]]
+            normed = raw_q[x][r].astype(F32) * inverse
+            back = unrotate(grad_q[x][rows], cos_ref[x, 0], sin_ref[x, 0])
+            sum_q = sum_q + jnp.sum(back * normed, axis=0, keepdims=True)
+            gq_ref[x, :, cols[r]] = norm_back(back * gain_q, normed, inverse).astype(BF16)
+            att_ref[x, :, cols[r]] = attended[x][rows].astype(BF16)
     for part in range(2):
         low, high = near_grad[0][part], near_grad[1][part]
         low_far, high_far = far_grad[0][part], far_grad[1][part]
@@ -200,7 +264,7 @@
     gains_ref[1:2, :] += sum_k
 
 
-def attend(group, device, doc_start, gain_q, gain_k, cosine, sine, queries, keys, values, cotangent, panels):
+def attend(group, device, doc_start, gain_q, gain_k, cosine, sine, queries, keys, values, cotangent, panels, prepared):
     block = queries.shape[1]
     width = gain_q.shape[0]
     heads = keys.shape[2] // width
@@ -228,13 +292,17 @@
             slim,
             slim,
             slim,
+            wide,
+            wide,
+            slim,
+            slim,
         ],
         out_specs=[wide, wide, slim, slim, slim, slim, slim, slim, whole((2, width))],
         out_shape=[
-            jax.ShapeDtypeStruct(queries.shape, BF16),
-            jax.ShapeDtypeStruct(queries.shape, BF16),
-            jax.ShapeDtypeStruct(keys.shape, F32),
-            jax.ShapeDtypeStruct(keys.shape, F32),
+            pltpu.HBM(queries.shape, BF16),
+            pltpu.HBM(queries.shape, BF16),
+            pltpu.HBM(keys.shape, F32),
+            pltpu.HBM(keys.shape, F32),
             pair,
             pair,
             pair,
@@ -243,42 +311,49 @@
         ],
         scratch_shapes=[pltpu.VMEM((2, PANELS * block, repeat * block), F32)],
         compiler_params=pltpu.CompilerParams(
-            dimension_semantics=("arbitrary",), vmem_limit_bytes=40 * 1024 * 1024
+            dimension_semantics=("arbitrary",), vmem_limit_bytes=32 * 1024 * 1024
         ),
         cost_estimate=pl.CostEstimate(
             flops=12 * pairs, bytes_accessed=12 * 1024 * 1024, transcendentals=pairs // width
         ),
         name="attend",
-    )(device, doc_start, gain_q[None], gain_k[None], cosine, sine, queries, keys, values, cotangent, *panels)
-
-
-def gather_kernel(group, index_ref, own_k_ref, own_v_ref, pair_ref, skip_ref, cross_ref, pay_ref, gk_ref, gv_ref):
+    )(device, doc_start, gain_q[None], gain_k[None], cosine, sine, *map(in_hbm, (queries, keys, values, cotangent)), *panels, *map(in_hbm, prepared))
+
+
+def gather_kernel(group, index_ref, own_k_ref, own_v_ref, cross_ref, skip_ref, pair_ref, pay_ref, gk_ref, gv_ref):
     device = index_ref[0]
     even = device % 2 == 0
     at_fold = device == group - 1
+    tile = own_k_ref.shape[1]
+    rows = pl.ds(pl.multiple_of(pl.program_id(0) * tile, tile), tile)
     for part, own_ref, out_ref in ((0, own_k_ref, gk_ref), (1, own_v_ref, gv_ref)):
-        direct = pair_ref[part].astype(F32) + skip_ref[part].astype(F32)
-        across = cross_ref[part].astype(F32) + jnp.where(at_fold, pay_ref[part].astype(F32), 0.0)
+        direct = pair_ref[part, rows].astype(F32) + skip_ref[part, rows].astype(F32)
+        across = cross_ref[part, rows].astype(F32)
+        across = across + jnp.where(at_fold, pay_ref[part, rows].astype(F32), 0.0)
         out_ref[0] = (own_ref[0] + jnp.where(even, direct, across)).astype(BF16)
         out_ref[1] = (own_ref[1] + jnp.where(even, across, direct)).astype(BF16)
 
 
 def gather(group, device, own_k, own_v, *arrived):
     _, block, columns = own_k.shape
-    tile = 256
-    spec = pl.BlockSpec((2, block, tile), lambda h: (0, 0, h))
+    tile = block // 4
+    spec = pl.BlockSpec((2, tile, columns), lambda h: (0, h, 0))
     return pl.pallas_call(
         functools.partial(gather_kernel, group),
-        grid=(columns // tile,),
-        in_specs=[pl.BlockSpec(memory_space=pltpu.SMEM)] + [spec] * 6,
+        grid=(block // tile,),
+        in_specs=[pl.BlockSpec(memory_space=pltpu.SMEM)]
+        + [spec] * 2
+        + [pl.BlockSpec(memory_space=pltpu.VMEM)] * 4,
         out_specs=[spec, spec],
-        out_shape=[jax.ShapeDtypeStruct(own_k.shape, BF16)] * 2,
-        compiler_params=pltpu.CompilerParams(dimension_semantics=("arbitrary",)),
+        out_shape=[pltpu.HBM(own_k.shape, BF16)] * 2,
+        compiler_params=pltpu.CompilerParams(
+            dimension_semantics=("arbitrary",), vmem_limit_bytes=32 * 1024 * 1024
+        ),
         cost_estimate=pl.CostEstimate(
             flops=8 * own_k.size, bytes_accessed=16 * own_k.size, transcendentals=0
         ),
         name="gather",
-    )(device, own_k, own_v, *arrived)
+    )(device, in_hbm(own_k), in_hbm(own_v), *arrived)
 
 
 def move(x, pairs):
@@ -317,7 +392,6 @@
     from_cross = move(second, cross)
     from_skip = move(first, skip_in)
     from_pair = move(first, pairs)
-    from_relay = move(jnp.where(at_fold, second, from_cross), pairs)
 
     rows = jnp.arange(block, dtype=jnp.int32)
     slots = jnp.stack([device, 2 * group - 1 - device])[:, None] - jnp.arange(PANELS)[None, :]
@@ -326,6 +400,9 @@
     sine = jnp.sin(angle)
     cosine = jnp.concatenate([cosine, cosine], axis=-1)
     sine = jnp.concatenate([-sine, sine], axis=-1)
+    prepared = prepare(gain_q, key_norm_gain, cosine[:, 0], sine[:, 0], queries, keys)
+    from_cross, *prepared = lax.optimization_barrier((from_cross, *prepared))
+    from_relay = move(jnp.where(at_fold, second, from_cross), pairs)
 
     attended, grad_queries, own_k, own_v, near_pair, near_cross, far_pair, far_cross, gains = attend(
         group,
@@ -340,16 +417,18 @@
         values,
         cotangent,
         (from_pair, from_cross, from_skip, from_relay),
+        prepared,
     )
     back_relay = move(far_pair, pairs)
+    pay = (near_cross.astype(F32) + back_relay.astype(F32)).astype(BF16)
+    near_pair, far_cross, pay = lax.optimization_barrier((near_pair, far_cross, pay))
+    back_cross = move(pay, cross)
+    back_skip = move(far_cross, skip_out)
     back_pair = move(near_pair, pairs)
-    back_skip = move(far_cross, skip_out)
-    pay = (near_cross.astype(F32) + back_relay.astype(F32)).astype(BF16)
-    back_cross = move(pay, cross)
     everyone = lax.axis_size("ctx") * lax.axis_size("dp")
     spread = jnp.broadcast_to(gains[None], (everyone,) + gains.shape)
     gains = jnp.sum(lax.all_to_all(spread, ("dp", "ctx"), 0, 0, tiled=True), axis=0)
-    grad_keys, grad_values = gather(group, index, own_k, own_v, back_pair, back_skip, back_cross, pay)
+    grad_keys, grad_values = gather(group, index, own_k, own_v, back_cross, back_skip, back_pair, pay)
     return attended, grad_queries, grad_keys, grad_values, gains[0], gains[1]
 
 

time: 86.3 us -> 76.4 us (0.89)
  waiting for transfers between devices: 17.7 us -> 12.7 us
  local copies, waits for them, and re-layouts: 6.96 us -> 2.57 us
  starting transfers between devices: 32.6 us -> 31.6 us
    pallas_call x1, Pallas kernels: 20.1 us -> 13.2 us  [attend(): pl.pallas_call(functools.partial(attend_kernel, group), grid=(heads,), in...]
    ppermute x8, waiting for transfers between devices: 11.8 us -> 5.02 us  [move(): return lax.ppermute(x, 'ctx', pairs)]
    pallas_call x1 -> x2, Pallas kernels: 4 us -> 10.7 us  [the longest x1 6.99 us: prepare(): pl.pallas_call(prepare_kernel, grid=(columns // width,), in_specs=[whole(...]
    unnamed x26 -> x6, local copies, waits for them, and re-layouts: 4.41 us -> 0.02 us
    all_to_all x1, waiting for transfers between devices: 5.88 us -> 7.73 us  [shards(): lax.all_to_all(spread, ('dp', 'ctx'), 0, 0, tiled=True)]
    convert_element_type x1, other arithmetic: 1.23 us -> 0.19 us  [shards(): pay = (near_cross.astype(F32) + back_relay.astype(F32)).astype(BF16)]
  transfers between devices with their start and end apart: 9 -> 9, of which waited for: 3 -> 3; matrix products, arithmetic and copies ran while one was open for 6% -> 6% of each run, Pallas kernels for 0% -> 9%
where the time goes in v3:
time: 76.4 us; the launch traced here: 75.9 us
  starting transfers between devices  31.6 us (41%)
  Pallas kernels  23.9 us (31%)
  waiting for transfers between devices  12.7 us (17%)
  other arithmetic  4.3 us (6%)
  local copies, waits for them, and re-layouts  2.57 us (3%)
  between operations  0.8 us (1%)
    ppermute x8, starting transfers between devices, move(): return lax.ppermute(x, 'ctx', pairs)  16.1 us
    all_to_all x1, starting transfers between devices, shards(): lax.all_to_all(spread, ('dp', 'ctx'), 0, 0, tiled=True)  15.4 us
    pallas_call x1, Pallas kernels, attend(): pl.pallas_call(functools.partial(attend_kernel, group), grid=(heads,), in...  13.2 us
    all_to_all x1, waiting for transfers between devices, shards(): lax.all_to_all(spread, ('dp', 'ctx'), 0, 0, tiled=True)  7.73 us
    pallas_call x1, Pallas kernels, prepare(): pl.pallas_call(prepare_kernel, grid=(columns // width,), in_specs=[whole(...  6.99 us
    ppermute x8, waiting for transfers between devices, move(): return lax.ppermute(x, 'ctx', pairs)  5.02 us
    pallas_call x1, Pallas kernels, gather(): pl.pallas_call(functools.partial(gather_kernel, group), grid=(block // ti...  3.7 us
  transfers between devices with their start and end apart: 9, of which 3 were waited for; matrix products, arithmetic and copies ran while one was open for 6% of the time, Pallas kernels for 9%

profile of v3, /device:TPU:1, one launch (start us, length us, event | category | flops | bytes accessed | tf_op | source)
XLA Modules:
  0.0 75.9 jit_solution(5095162017483540313)
XLA Ops:
  0.6 1.3 %fusion.7 = (bf16[1,128,1024]{2,1,0:T(8,128)(2,1)S(1)}, bf16[1,128,1024]{2,1,0:T(8,128)(2,1)S(1)}, bf16[1,128,1024]{2,1,0:T(8,128)(2,1)S(1)}, bf16[1,128,1024]{2,1,0:T(8,128)(2,1)S(1)}) fusion(bf16[2,128,1024]{2,1,0:T(8,128)(2,1)} %k_ref.3, bf16[2,128,1024]{2,1,0:T(8,128)(2,1)} %v_ref.1), kind=kLoop, calls=%fused_computation.29 | loop fusion | bytes 2097152 | tf_op jit(solution)/shard_map/slice | solution.py:388
  1.9 0.9 %broadcast_select_fusion.1 = (bf16[2,128,1024]{2,1,0:T(8,128)(2,1)S(1)}, bf16[2,128,1024]{2,1,0:T(8,128)(2,1)}) fusion(pred[]{:T(512)S(6)} %eq.8, bf16[1,128,1024]{2,1,0:T(8,128)(2,1)S(1)} %get-tuple-element.71, bf16[1,128,1024]{2,1,0:T(8,128)(2,1)S(1)} %get-tuple-element.55, bf16[1,128,1024]{2,1,0:T(8,128)(2,1)S(1)} %get-tuple-element.72, ...), kind=kLoop, calls=%fused_computation.6 | loop fusion | flops 1048576 | bytes 2097153 | tf_op jit(solution)/shard_map/jit(_where)/select_n | solution.py:391
  2.8 1.3 %collective-permute-start.2 = (bf16[2,128,1024]{2,1,0:T(8,128)(2,1)}, bf16[2,128,1024]{2,1,0:T(8,128)(2,1)S(1)}, u32[]{:S(2)}, u32[]{:S(2)}) collective-permute-start(bf16[2,128,1024]{2,1,0:T(8,128)(2,1)} %get-tuple-element.53), channel_id=1, source_target_pairs={{0,2},{2,4},{4,6},{6,8},{8,10},{10,12},{12,14},{14,16},{16,18},{18... | collective-permute-start | bytes 1572872 | tf_op jit(solution)/shard_map/ppermute | solution.py:360
  4.1 3.8 %collective-permute-start = (bf16[2,128,1024]{2,1,0:T(8,128)(2,1)}, bf16[2,128,1024]{2,1,0:T(8,128)(2,1)S(1)}, u32[]{:S(2)}, u32[]{:S(2)}) collective-permute-start(bf16[2,128,1024]{2,1,0:T(8,128)(2,1)} %get-tuple-element.53), channel_id=1, source_target_pairs={{0,1},{1,0},{2,3},{3,2},{4,5},{5,4},{6,7},{7,6},{8,9},{9,8},{10,11... | collective-permute-start | bytes 1572872 | tf_op jit(solution)/shard_map/ppermute | solution.py:360
  7.9 3.1 %collective-permute-start.1 = (bf16[2,128,1024]{2,1,0:T(8,128)(2,1)S(1)}, bf16[2,128,1024]{2,1,0:T(8,128)(2,1)S(1)}, u32[]{:S(2)}, u32[]{:S(2)}) collective-permute-start(bf16[2,128,1024]{2,1,0:T(8,128)(2,1)S(1)} %get-tuple-element.52), channel_id=1, source_target_pairs={{1,2},{3,4},{5,6},{7,8},{9,10},{11,12},{13,14},{15,16},{17,18},{19... | collective-permute-start | bytes 1572872 | tf_op jit(solution)/shard_map/ppermute | solution.py:360
  11.0 0.1 pad_add_fusion
  11.1 0.1 compare_and_fusion
  11.1 0.1 fusion.6
  11.2 0.1 select_convert_fusion
  11.3 1.5 %fusion.4 = (f32[2,3,128,64]{3,2,1,0:T(8,128)S(1)}, f32[2,3,128,64]{3,2,1,0:T(8,128)S(1)}, f32[2,3,128,64]{3,2,1,0:T(8,128)S(1)}) fusion(f32[64]{0:T(128)S(1)} %multiply_exponential_fusion, f32[2,3,128]{2,1,0:T(4,128)S(1)} %select_convert_fusion), kind=kLoop, calls=%fused_computation.18 | loop fusion | flops 98304 | bytes 593152 | tf_op jit(solution)/shard_map/neg | solution.py:402
  12.8 0.8 %fusion.1 = (f32[2,128,128]{2,1,0:T(8,128)}, f32[2,128,128]{2,1,0:T(8,128)}) fusion(f32[2,3,128,64]{3,2,1,0:T(8,128)S(1)} %get-tuple-element.58, f32[2,3,128,64]{3,2,1,0:T(8,128)S(1)} %get-tuple-element.59, f32[2,3,128,64]{3,2,1,0:T(8,128)S(1)} %get-tuple-element.60), kind=kLoop, calls=%fused_computation.15 | loop fusion | flops 65536 | bytes 851968 | tf_op jit(solution)/shard_map/squeeze | solution.py:403
  13.6 7.0 %prepare.1 = (bf16[2,128,2048]{2,1,0:T(8,128)(2,1)}, f32[2,128,2048]{2,1,0:T(8,128)}, bf16[2,128,1024]{2,1,0:T(8,128)(2,1)}, f32[2,128,1024]{2,1,0:T(8,128)}) custom-call(f32[1,128]{1,0:T(1,128)} %bitcast.12, f32[1,128]{1,0:T(1,128)} %bitcast.14, f32[2,128,128]{2,1,0:T(8,128)} %get-tuple-element.70.cos_ref, f32[2,128,128]{2,1,0:T(8,128)} %get-tuple-element.69.sin_ref, ...), custom_call_target="tpu_custom_call" | custom-call | flops 33554432 | bytes 8388608 | tf_op jit(solution)/shard_map/prepare/pallas_call | solution.py:94
  20.6 0.0 copy-start
  20.6 0.0 copy-start.1
  20.6 0.0 copy-start.2
  20.6 0.1 broadcast_select_fusion
  20.7 0.1 collective-permute-start.3
  20.8 0.3 pad_maximum_fusion.2
  21.1 1.6 %collective-permute-done.3.relay_ref = bf16[2,128,1024]{2,1,0:T(8,128)(2,1)S(1)} collective-permute-done((bf16[2,128,1024]{2,1,0:T(8,128)(2,1)S(1)}, bf16[2,128,1024]{2,1,0:T(8,128)(2,1)S(1)}, u32[]{:S(2)}, u32[]{:S(2)}) %collective-permute-start.3) | collective-permute-done | bytes 524320 | tf_op jit(solution)/shard_map/ppermute | solution.py:360
  22.7 13.2 %attend.1 = (bf16[2,128,2048]{2,1,0:T(8,128)(2,1)}, bf16[2,128,2048]{2,1,0:T(8,128)(2,1)}, f32[2,128,1024]{2,1,0:T(8,128)}, f32[2,128,1024]{2,1,0:T(8,128)}, bf1...) custom-call(s32[1]{0:T(128)} %bitcast.index_ref, ...), custom_call_target="tpu_custom_call" | custom-call | flops 2415919104 | bytes 12582912 | tf_op jit(solution)/shard_map/attend/pallas_call | solution.py:277
  35.9 0.2 collective-permute-start.4
  36.1 0.8 %broadcast_in_dim.50 = f32[256,2,128]{2,1,0:T(2,128)} broadcast(f32[2,128]{1,0:T(2,128)S(1)} %get-tuple-element.51), dimensions={1,2} | broadcast | bytes 263168 | tf_op jit(solution)/shard_map/broadcast_in_dim | solution.py:429
  36.9 15.4 %all-to-all-start = ((f32[256,2,128]{2,1,0:T(2,128)}), f32[256,2,128]{2,1,0:T(2,128)S(1)}, u32[]{:S(2)}, u32[]{:S(2)}) async-start(f32[256,2,128]{2,1,0:T(2,128)} %broadcast_in_dim.50), calls=%async_computation | async-start | bytes 524288 | tf_op jit(solution)/shard_map/all_to_all | solution.py:430
  52.3 0.2 add_convert_fusion.pay_ref
  52.5 3.3 %collective-permute-start.6 = (bf16[2,128,1024]{2,1,0:T(8,128)(2,1)S(1)}, bf16[2,128,1024]{2,1,0:T(8,128)(2,1)S(1)}, u32[]{:S(2)}, u32[]{:S(2)}) collective-permute-start(bf16[2,128,1024]{2,1,0:T(8,128)(2,1)S(1)} %get-tuple-element.47), channel_id=1, source_target_pairs={{2,0},{4,2},{6,4},{8,6},{10,8},{12,10},{14,12},{16,14},{18,16},{20... | collective-permute-start | bytes 1572872 | tf_op jit(solution)/shard_map/ppermute | solution.py:360
  55.9 0.2 collective-permute-start.7
  56.1 4.2 %collective-permute-start.5 = (bf16[2,128,1024]{2,1,0:T(8,128)(2,1)S(1)}, bf16[2,128,1024]{2,1,0:T(8,128)(2,1)S(1)}, u32[]{:S(2)}, u32[]{:S(2)}) collective-permute-start(bf16[2,128,1024]{2,1,0:T(8,128)(2,1)S(1)} %add_convert_fusion.pay_ref), channel_id=1, source_target_pairs={{1,2},{3,4},{5,6},{7,8},{9,10},{11,12},{13,14},{15,16},{17,18},{19... | collective-permute-start | bytes 1572872 | tf_op jit(solution)/shard_map/ppermute | solution.py:360
  60.2 7.7 %all-to-all-done = f32[256,2,128]{2,1,0:T(2,128)S(1)} async-done(((f32[256,2,128]{2,1,0:T(2,128)}), f32[256,2,128]{2,1,0:T(2,128)S(1)}, u32[]{:S(2)}, u32[]{:S(2)}) %all-to-all-start) | async-done | bytes 262176 | tf_op jit(solution)/shard_map/all_to_all | solution.py:430
  68.0 0.3 reduce_sum.9
  68.2 0.5 slice_bitcast_fusion
  68.8 3.4 %collective-permute-done.5.cross_ref = bf16[2,128,1024]{2,1,0:T(8,128)(2,1)S(1)} collective-permute-done((bf16[2,128,1024]{2,1,0:T(8,128)(2,1)S(1)}, bf16[2,128,1024]{2,1,0:T(8,128)(2,1)S(1)}, u32[]{:S(2)}, u32[]{:S(2)}) %collective-permute-start.5) | collective-permute-done | bytes 524320 | tf_op jit(solution)/shard_map/ppermute | solution.py:360
  72.2 3.7 %gather.1 = (bf16[2,128,1024]{2,1,0:T(8,128)(2,1)}, bf16[2,128,1024]{2,1,0:T(8,128)(2,1)}) custom-call(s32[1]{0:T(128)} %bitcast.index_ref, f32[2,128,1024]{2,1,0:T(8,128)} %get-tuple-element.40.own_k_ref, f32[2,128,1024]{2,1,0:T(8,128)} %get-tuple-element.41.own_v_ref, bf16[2,128,1024]{2,1,0:T(8,128)(2,1)S(1)} %collective-permute-done.5.cross_ref, ...), custom_call_target="tpu_custom_call" | custom-call | flops 2097152 | bytes 4194304 | tf_op jit(solution)/shard_map/gather/pallas_call | solution.py:341
  (10 shorter events, 0.0 us)
Async XLA Ops:
  2.8 18.3 %collective-permute-start.2 = (bf16[2,128,1024]{2,1,0:T(8,128)(2,1)}, bf16[2,128,1024]{2,1,0:T(8,128)(2,1)S(1)}, u32[]{:S(2)}, u32[]{:S(2)}) collective-permute-start(bf16[2,128,1024]{2,1,0:T(8,128)(2,1)} %get-tuple-element.53), channel_id=1, source_target_pairs={{0,2},{2,4},{4,6},{6,8},{8,10},{10,12},{12,14},{14,16},{16,18},{18... | collective-permute-start | bytes 1572872 | tf_op jit(solution)/shard_map/ppermute | solution.py:360
  4.1 17.0 %collective-permute-start = (bf16[2,128,1024]{2,1,0:T(8,128)(2,1)}, bf16[2,128,1024]{2,1,0:T(8,128)(2,1)S(1)}, u32[]{:S(2)}, u32[]{:S(2)}) collective-permute-start(bf16[2,128,1024]{2,1,0:T(8,128)(2,1)} %get-tuple-element.53), channel_id=1, source_target_pairs={{0,1},{1,0},{2,3},{3,2},{4,5},{5,4},{6,7},{7,6},{8,9},{9,8},{10,11... | collective-permute-start | bytes 1572872 | tf_op jit(solution)/shard_map/ppermute | solution.py:360
  7.9 12.7 %collective-permute-start.1 = (bf16[2,128,1024]{2,1,0:T(8,128)(2,1)S(1)}, bf16[2,128,1024]{2,1,0:T(8,128)(2,1)S(1)}, u32[]{:S(2)}, u32[]{:S(2)}) collective-permute-start(bf16[2,128,1024]{2,1,0:T(8,128)(2,1)S(1)} %get-tuple-element.52), channel_id=1, source_target_pairs={{1,2},{3,4},{5,6},{7,8},{9,10},{11,12},{13,14},{15,16},{17,18},{19... | collective-permute-start | bytes 1572872 | tf_op jit(solution)/shard_map/ppermute | solution.py:360
  20.6 2.1 %copy-start = (f32[128]{0:T(128)S(1)}, f32[128]{0:T(128)}, u32[]{:S(2)}) copy-start(f32[128]{0:T(128)} %param.11) | copy-start | bytes 1540
  20.6 2.1 %copy-start.1 = (f32[128]{0:T(128)S(1)}, f32[128]{0:T(128)}, u32[]{:S(2)}) copy-start(f32[128]{0:T(128)} %param.12) | copy-start | bytes 1540
  20.6 2.1 %copy-start.2 = (s32[2,128]{1,0:T(2,128)S(1)}, s32[2,128]{1,0:T(2,128)}, u32[]{:S(2)}) copy-start(s32[2,128]{1,0:T(2,128)} %doc_ref.1) | copy-start | bytes 3076
  20.7 2.0 %collective-permute-start.3 = (bf16[2,128,1024]{2,1,0:T(8,128)(2,1)S(1)}, bf16[2,128,1024]{2,1,0:T(8,128)(2,1)S(1)}, u32[]{:S(2)}, u32[]{:S(2)}) collective-permute-start(bf16[2,128,1024]{2,1,0:T(8,128)(2,1)S(1)} %broadcast_select_fusion), channel_id=1, source_target_pairs={{0,1},{1,0},{2,3},{3,2},{4,5},{5,4},{6,7},{7,6},{8,9},{9,8},{10,11... | collective-permute-start | bytes 1572872 | tf_op jit(solution)/shard_map/ppermute | solution.py:360
  35.9 16.4 %collective-permute-start.4 = (bf16[2,128,1024]{2,1,0:T(8,128)(2,1)}, bf16[2,128,1024]{2,1,0:T(8,128)(2,1)S(1)}, u32[]{:S(2)}, u32[]{:S(2)}) collective-permute-start(bf16[2,128,1024]{2,1,0:T(8,128)(2,1)} %get-tuple-element.45), channel_id=1, source_target_pairs={{0,1},{1,0},{2,3},{3,2},{4,5},{5,4},{6,7},{7,6},{8,9},{9,8},{10,11... | collective-permute-start | bytes 1572872 | tf_op jit(solution)/shard_map/ppermute | solution.py:360
  36.9 31.1 %all-to-all-start = ((f32[256,2,128]{2,1,0:T(2,128)}), f32[256,2,128]{2,1,0:T(2,128)S(1)}, u32[]{:S(2)}, u32[]{:S(2)}) async-start(f32[256,2,128]{2,1,0:T(2,128)} %broadcast_in_dim.50), calls=%async_computation | async-start | bytes 524288 | tf_op jit(solution)/shard_map/all_to_all | solution.py:430
  52.5 16.2 %collective-permute-start.6 = (bf16[2,128,1024]{2,1,0:T(8,128)(2,1)S(1)}, bf16[2,128,1024]{2,1,0:T(8,128)(2,1)S(1)}, u32[]{:S(2)}, u32[]{:S(2)}) collective-permute-start(bf16[2,128,1024]{2,1,0:T(8,128)(2,1)S(1)} %get-tuple-element.47), channel_id=1, source_target_pairs={{2,0},{4,2},{6,4},{8,6},{10,8},{12,10},{14,12},{16,14},{18,16},{20... | collective-permute-start | bytes 1572872 | tf_op jit(solution)/shard_map/ppermute | solution.py:360
  55.9 12.9 %collective-permute-start.7 = (bf16[2,128,1024]{2,1,0:T(8,128)(2,1)S(1)}, bf16[2,128,1024]{2,1,0:T(8,128)(2,1)S(1)}, u32[]{:S(2)}, u32[]{:S(2)}) collective-permute-start(bf16[2,128,1024]{2,1,0:T(8,128)(2,1)S(1)} %get-tuple-element.48), channel_id=1, source_target_pairs={{0,1},{1,0},{2,3},{3,2},{4,5},{5,4},{6,7},{7,6},{8,9},{9,8},{10,11... | collective-permute-start | bytes 1572872 | tf_op jit(solution)/shard_map/ppermute | solution.py:360
  56.1 16.1 %collective-permute-start.5 = (bf16[2,128,1024]{2,1,0:T(8,128)(2,1)S(1)}, bf16[2,128,1024]{2,1,0:T(8,128)(2,1)S(1)}, u32[]{:S(2)}, u32[]{:S(2)}) collective-permute-start(bf16[2,128,1024]{2,1,0:T(8,128)(2,1)S(1)} %add_convert_fusion.pay_ref), channel_id=1, source_target_pairs={{1,2},{3,4},{5,6},{7,8},{9,10},{11,12},{13,14},{15,16},{17,18},{19... | collective-permute-start | bytes 1572872 | tf_op jit(solution)/shard_map/ppermute | solution.py:360

commit v4 on v3

--- a/solution.py
+++ b/solution.py
@@ -320,30 +320,28 @@
     )(device, doc_start, gain_q[None], gain_k[None], cosine, sine, *map(in_hbm, (queries, keys, values, cotangent)), *panels, *map(in_hbm, prepared))
 
 
-def gather_kernel(group, index_ref, own_k_ref, own_v_ref, cross_ref, skip_ref, pair_ref, pay_ref, gk_ref, gv_ref):
+def gather_kernel(index_ref, own_k_ref, own_v_ref, cross_ref, skip_ref, pair_ref, gk_ref, gv_ref):
     device = index_ref[0]
     even = device % 2 == 0
-    at_fold = device == group - 1
     tile = own_k_ref.shape[1]
     rows = pl.ds(pl.multiple_of(pl.program_id(0) * tile, tile), tile)
     for part, own_ref, out_ref in ((0, own_k_ref, gk_ref), (1, own_v_ref, gv_ref)):
         direct = pair_ref[part, rows].astype(F32) + skip_ref[part, rows].astype(F32)
-        across = cross_ref[part, rows].astype(F32)
-        across = across + jnp.where(at_fold, pay_ref[part, rows].astype(F32), 0.0)
+        across = cross_ref[part, rows]
         out_ref[0] = (own_ref[0] + jnp.where(even, direct, across)).astype(BF16)
         out_ref[1] = (own_ref[1] + jnp.where(even, across, direct)).astype(BF16)
 
 
-def gather(group, device, own_k, own_v, *arrived):
+def gather(device, own_k, own_v, *arrived):
     _, block, columns = own_k.shape
-    tile = block // 4
+    tile = block // 2
     spec = pl.BlockSpec((2, tile, columns), lambda h: (0, h, 0))
     return pl.pallas_call(
-        functools.partial(gather_kernel, group),
+        gather_kernel,
         grid=(block // tile,),
         in_specs=[pl.BlockSpec(memory_space=pltpu.SMEM)]
         + [spec] * 2
-        + [pl.BlockSpec(memory_space=pltpu.VMEM)] * 4,
+        + [pl.BlockSpec(memory_space=pltpu.VMEM)] * 3,
         out_specs=[spec, spec],
         out_shape=[pltpu.HBM(own_k.shape, BF16)] * 2,
         compiler_params=pltpu.CompilerParams(
@@ -428,7 +426,8 @@
     everyone = lax.axis_size("ctx") * lax.axis_size("dp")
     spread = jnp.broadcast_to(gains[None], (everyone,) + gains.shape)
     gains = jnp.sum(lax.all_to_all(spread, ("dp", "ctx"), 0, 0, tiled=True), axis=0)
-    grad_keys, grad_values = gather(group, index, own_k, own_v, back_cross, back_skip, back_pair, pay)
+    across = back_cross.astype(F32) + jnp.where(at_fold, pay.astype(F32), 0.0)
+    grad_keys, grad_values = gather(index, own_k, own_v, across, back_skip, back_pair)
     return attended, grad_queries, grad_keys, grad_values, gains[0], gains[1]
 
 

time: 76.4 us -> 74.9 us (0.980)
  the two profiles are of different devices: /device:TPU:1 before, /device:TPU:33 now
where the time goes in v4:
time: 74.9 us; the launch traced here: 74.4 us
  starting transfers between devices  30.8 us (41%)
  Pallas kernels  22.6 us (30%)
  waiting for transfers between devices  13.2 us (18%)
  other arithmetic  4.48 us (6%)
  local copies, waits for them, and re-layouts  2.57 us (3%)
  between operations  0.81 us (1%)
    ppermute x8, starting transfers between devices, move(): return lax.ppermute(x, 'ctx', pairs)  18 us
    pallas_call x1, Pallas kernels, attend(): pl.pallas_call(functools.partial(attend_kernel, group), grid=(heads,), in...  13.2 us
    all_to_all x1, starting transfers between devices, shards(): lax.all_to_all(spread, ('dp', 'ctx'), 0, 0, tiled=True)  12.7 us
    all_to_all x1, waiting for transfers between devices, shards(): lax.all_to_all(spread, ('dp', 'ctx'), 0, 0, tiled=True)  7.18 us
    pallas_call x1, Pallas kernels, prepare(): pl.pallas_call(prepare_kernel, grid=(columns // width,), in_specs=[whole(...  6.98 us
    ppermute x8, waiting for transfers between devices, move(): return lax.ppermute(x, 'ctx', pairs)  6.01 us
    pallas_call x1, Pallas kernels, gather(): pl.pallas_call(gather_kernel, grid=(block // tile,), in_specs=[pl.BlockSp...  2.5 us
  transfers between devices with their start and end apart: 9, of which 3 were waited for; matrix products, arithmetic and copies ran while one was open for 7% of the time, Pallas kernels for 9%

profile of v4, /device:TPU:33, one launch (start us, length us, event | category | flops | bytes accessed | tf_op | source)
XLA Modules:
  0.0 74.4 jit_solution(7960390122122286047)
XLA Ops:
  0.6 1.3 %fusion.7 = (bf16[1,128,1024]{2,1,0:T(8,128)(2,1)S(1)}, bf16[1,128,1024]{2,1,0:T(8,128)(2,1)S(1)}, bf16[1,128,1024]{2,1,0:T(8,128)(2,1)S(1)}, bf16[1,128,1024]{2,1,0:T(8,128)(2,1)S(1)}) fusion(bf16[2,128,1024]{2,1,0:T(8,128)(2,1)} %k_ref.3, bf16[2,128,1024]{2,1,0:T(8,128)(2,1)} %v_ref.1), kind=kLoop, calls=%fused_computation.30 | loop fusion | bytes 2097152 | tf_op jit(solution)/shard_map/slice | solution.py:386
  1.9 0.9 %broadcast_select_fusion.1 = (bf16[2,128,1024]{2,1,0:T(8,128)(2,1)S(1)}, bf16[2,128,1024]{2,1,0:T(8,128)(2,1)}) fusion(pred[]{:T(512)S(6)} %eq.8, bf16[1,128,1024]{2,1,0:T(8,128)(2,1)S(1)} %get-tuple-element.71, bf16[1,128,1024]{2,1,0:T(8,128)(2,1)S(1)} %get-tuple-element.55, bf16[1,128,1024]{2,1,0:T(8,128)(2,1)S(1)} %get-tuple-element.72, ...), kind=kLoop, calls=%fused_computation.7 | loop fusion | flops 1048576 | bytes 2097153 | tf_op jit(solution)/shard_map/jit(_where)/select_n | solution.py:389
  2.8 4.2 %collective-permute-start.2 = (bf16[2,128,1024]{2,1,0:T(8,128)(2,1)}, bf16[2,128,1024]{2,1,0:T(8,128)(2,1)S(1)}, u32[]{:S(2)}, u32[]{:S(2)}) collective-permute-start(bf16[2,128,1024]{2,1,0:T(8,128)(2,1)} %get-tuple-element.53), channel_id=1, source_target_pairs={{0,2},{2,4},{4,6},{6,8},{8,10},{10,12},{12,14},{14,16},{16,18},{18... | collective-permute-start | bytes 1572872 | tf_op jit(solution)/shard_map/ppermute | solution.py:358
  7.0 0.1 collective-permute-start
  7.1 3.1 %collective-permute-start.1 = (bf16[2,128,1024]{2,1,0:T(8,128)(2,1)S(1)}, bf16[2,128,1024]{2,1,0:T(8,128)(2,1)S(1)}, u32[]{:S(2)}, u32[]{:S(2)}) collective-permute-start(bf16[2,128,1024]{2,1,0:T(8,128)(2,1)S(1)} %get-tuple-element.52), channel_id=1, source_target_pairs={{1,2},{3,4},{5,6},{7,8},{9,10},{11,12},{13,14},{15,16},{17,18},{19... | collective-permute-start | bytes 1572872 | tf_op jit(solution)/shard_map/ppermute | solution.py:358
  10.2 0.1 pad_add_fusion
  10.2 0.1 compare_and_fusion
  10.3 0.1 fusion.6
  10.4 0.1 select_convert_fusion
  10.5 1.5 %fusion.4 = (f32[2,3,128,64]{3,2,1,0:T(8,128)S(1)}, f32[2,3,128,64]{3,2,1,0:T(8,128)S(1)}, f32[2,3,128,64]{3,2,1,0:T(8,128)S(1)}) fusion(f32[64]{0:T(128)S(1)} %multiply_exponential_fusion, f32[2,3,128]{2,1,0:T(4,128)S(1)} %select_convert_fusion), kind=kLoop, calls=%fused_computation.19 | loop fusion | flops 98304 | bytes 593152 | tf_op jit(solution)/shard_map/neg | solution.py:400
  11.9 0.8 %fusion.1 = (f32[2,128,128]{2,1,0:T(8,128)}, f32[2,128,128]{2,1,0:T(8,128)}) fusion(f32[2,3,128,64]{3,2,1,0:T(8,128)S(1)} %get-tuple-element.58, f32[2,3,128,64]{3,2,1,0:T(8,128)S(1)} %get-tuple-element.59, f32[2,3,128,64]{3,2,1,0:T(8,128)S(1)} %get-tuple-element.60), kind=kLoop, calls=%fused_computation.16 | loop fusion | flops 65536 | bytes 851968 | tf_op jit(solution)/shard_map/squeeze | solution.py:401
  12.8 7.0 %prepare.1 = (bf16[2,128,2048]{2,1,0:T(8,128)(2,1)}, f32[2,128,2048]{2,1,0:T(8,128)}, bf16[2,128,1024]{2,1,0:T(8,128)(2,1)}, f32[2,128,1024]{2,1,0:T(8,128)}) custom-call(f32[1,128]{1,0:T(1,128)} %bitcast.12, f32[1,128]{1,0:T(1,128)} %bitcast.14, f32[2,128,128]{2,1,0:T(8,128)} %get-tuple-element.70.cos_ref, f32[2,128,128]{2,1,0:T(8,128)} %get-tuple-element.69.sin_ref, ...), custom_call_target="tpu_custom_call" | custom-call | flops 33554432 | bytes 8388608 | tf_op jit(solution)/shard_map/prepare/pallas_call | solution.py:94
  19.8 0.0 copy-start.1
  19.8 0.0 copy-start.2
  19.8 0.1 broadcast_select_fusion
  19.9 2.8 %collective-permute-start.3 = (bf16[2,128,1024]{2,1,0:T(8,128)(2,1)S(1)}, bf16[2,128,1024]{2,1,0:T(8,128)(2,1)S(1)}, u32[]{:S(2)}, u32[]{:S(2)}) collective-permute-start(bf16[2,128,1024]{2,1,0:T(8,128)(2,1)S(1)} %broadcast_select_fusion), channel_id=1, source_target_pairs={{0,1},{1,0},{2,3},{3,2},{4,5},{5,4},{6,7},{7,6},{8,9},{9,8},{10,11... | collective-permute-start | bytes 1572872 | tf_op jit(solution)/shard_map/ppermute | solution.py:358
  22.6 0.3 pad_maximum_fusion.2
  22.9 1.2 %collective-permute-done.3.relay_ref = bf16[2,128,1024]{2,1,0:T(8,128)(2,1)S(1)} collective-permute-done((bf16[2,128,1024]{2,1,0:T(8,128)(2,1)S(1)}, bf16[2,128,1024]{2,1,0:T(8,128)(2,1)S(1)}, u32[]{:S(2)}, u32[]{:S(2)}) %collective-permute-start.3) | collective-permute-done | bytes 524320 | tf_op jit(solution)/shard_map/ppermute | solution.py:358
  24.2 13.2 %attend.1 = (bf16[2,128,2048]{2,1,0:T(8,128)(2,1)}, bf16[2,128,2048]{2,1,0:T(8,128)(2,1)}, f32[2,128,1024]{2,1,0:T(8,128)}, f32[2,128,1024]{2,1,0:T(8,128)}, bf1...) custom-call(s32[1]{0:T(128)} %bitcast.index_ref, ...), custom_call_target="tpu_custom_call" | custom-call | flops 2415919104 | bytes 12582912 | tf_op jit(solution)/shard_map/attend/pallas_call | solution.py:277
  37.3 0.5 collective-permute-start.4
  37.8 0.8 %broadcast_in_dim.55 = f32[256,2,128]{2,1,0:T(2,128)} broadcast(f32[2,128]{1,0:T(2,128)S(1)} %get-tuple-element.51), dimensions={1,2} | broadcast | bytes 263168 | tf_op jit(solution)/shard_map/broadcast_in_dim | solution.py:427
  38.6 12.7 %all-to-all-start = ((f32[256,2,128]{2,1,0:T(2,128)}), f32[256,2,128]{2,1,0:T(2,128)S(1)}, u32[]{:S(2)}, u32[]{:S(2)}) async-start(f32[256,2,128]{2,1,0:T(2,128)} %broadcast_in_dim.55), calls=%async_computation | async-start | bytes 524288 | tf_op jit(solution)/shard_map/all_to_all | solution.py:428
  51.4 0.2 add_convert_fusion
  51.6 3.4 %collective-permute-start.5 = (bf16[2,128,1024]{2,1,0:T(8,128)(2,1)S(1)}, bf16[2,128,1024]{2,1,0:T(8,128)(2,1)S(1)}, u32[]{:S(2)}, u32[]{:S(2)}) collective-permute-start(bf16[2,128,1024]{2,1,0:T(8,128)(2,1)S(1)} %add_convert_fusion), channel_id=1, source_target_pairs={{1,2},{3,4},{5,6},{7,8},{9,10},{11,12},{13,14},{15,16},{17,18},{19... | collective-permute-start | bytes 1572872 | tf_op jit(solution)/shard_map/ppermute | solution.py:358
  55.0 3.2 %collective-permute-start.6 = (bf16[2,128,1024]{2,1,0:T(8,128)(2,1)S(1)}, bf16[2,128,1024]{2,1,0:T(8,128)(2,1)S(1)}, u32[]{:S(2)}, u32[]{:S(2)}) collective-permute-start(bf16[2,128,1024]{2,1,0:T(8,128)(2,1)S(1)} %get-tuple-element.47), channel_id=1, source_target_pairs={{2,0},{4,2},{6,4},{8,6},{10,8},{12,10},{14,12},{16,14},{18,16},{20... | collective-permute-start | bytes 1572872 | tf_op jit(solution)/shard_map/ppermute | solution.py:358
  58.1 0.9 %collective-permute-start.7 = (bf16[2,128,1024]{2,1,0:T(8,128)(2,1)S(1)}, bf16[2,128,1024]{2,1,0:T(8,128)(2,1)S(1)}, u32[]{:S(2)}, u32[]{:S(2)}) collective-permute-start(bf16[2,128,1024]{2,1,0:T(8,128)(2,1)S(1)} %get-tuple-element.48), channel_id=1, source_target_pairs={{0,1},{1,0},{2,3},{3,2},{4,5},{5,4},{6,7},{7,6},{8,9},{9,8},{10,11... | collective-permute-start | bytes 1572872 | tf_op jit(solution)/shard_map/ppermute | solution.py:358
  59.0 7.2 %all-to-all-done = f32[256,2,128]{2,1,0:T(2,128)S(1)} async-done(((f32[256,2,128]{2,1,0:T(2,128)}), f32[256,2,128]{2,1,0:T(2,128)S(1)}, u32[]{:S(2)}, u32[]{:S(2)}) %all-to-all-start) | async-done | bytes 262176 | tf_op jit(solution)/shard_map/all_to_all | solution.py:428
  66.2 0.3 reduce_sum.9
  66.5 0.5 slice_bitcast_fusion
  67.0 0.2 select_add_fusion.cross_ref
  67.2 4.7 %collective-permute-done.6.skip_ref = bf16[2,128,1024]{2,1,0:T(8,128)(2,1)S(1)} collective-permute-done((bf16[2,128,1024]{2,1,0:T(8,128)(2,1)S(1)}, bf16[2,128,1024]{2,1,0:T(8,128)(2,1)S(1)}, u32[]{:S(2)}, u32[]{:S(2)}) %collective-permute-start.6) | collective-permute-done | bytes 524320 | tf_op jit(solution)/shard_map/ppermute | solution.py:358
  71.9 2.5 %gather.1 = (bf16[2,128,1024]{2,1,0:T(8,128)(2,1)}, bf16[2,128,1024]{2,1,0:T(8,128)(2,1)}) custom-call(s32[1]{0:T(128)} %bitcast.index_ref, f32[2,128,1024]{2,1,0:T(8,128)} %get-tuple-element.40.own_k_ref, f32[2,128,1024]{2,1,0:T(8,128)} %get-tuple-element.41.own_v_ref, f32[2,128,1024]{2,1,0:T(8,128)S(1)} %select_add_fusion.cross_ref, ...), custom_call_target="tpu_custom_call" | custom-call | flops 2097152 | bytes 4194304 | tf_op jit(solution)/shard_map/gather/pallas_call | solution.py:339
  (11 shorter events, 0.0 us)
Async XLA Ops:
  2.8 20.1 %collective-permute-start.2 = (bf16[2,128,1024]{2,1,0:T(8,128)(2,1)}, bf16[2,128,1024]{2,1,0:T(8,128)(2,1)S(1)}, u32[]{:S(2)}, u32[]{:S(2)}) collective-permute-start(bf16[2,128,1024]{2,1,0:T(8,128)(2,1)} %get-tuple-element.53), channel_id=1, source_target_pairs={{0,2},{2,4},{4,6},{6,8},{8,10},{10,12},{12,14},{14,16},{16,18},{18... | collective-permute-start | bytes 1572872 | tf_op jit(solution)/shard_map/ppermute | solution.py:358
  7.0 15.9 %collective-permute-start = (bf16[2,128,1024]{2,1,0:T(8,128)(2,1)}, bf16[2,128,1024]{2,1,0:T(8,128)(2,1)S(1)}, u32[]{:S(2)}, u32[]{:S(2)}) collective-permute-start(bf16[2,128,1024]{2,1,0:T(8,128)(2,1)} %get-tuple-element.53), channel_id=1, source_target_pairs={{0,1},{1,0},{2,3},{3,2},{4,5},{5,4},{6,7},{7,6},{8,9},{9,8},{10,11... | collective-permute-start | bytes 1572872 | tf_op jit(solution)/shard_map/ppermute | solution.py:358
  7.1 12.7 %collective-permute-start.1 = (bf16[2,128,1024]{2,1,0:T(8,128)(2,1)S(1)}, bf16[2,128,1024]{2,1,0:T(8,128)(2,1)S(1)}, u32[]{:S(2)}, u32[]{:S(2)}) collective-permute-start(bf16[2,128,1024]{2,1,0:T(8,128)(2,1)S(1)} %get-tuple-element.52), channel_id=1, source_target_pairs={{1,2},{3,4},{5,6},{7,8},{9,10},{11,12},{13,14},{15,16},{17,18},{19... | collective-permute-start | bytes 1572872 | tf_op jit(solution)/shard_map/ppermute | solution.py:358
  19.8 4.4 %copy-start = (f32[128]{0:T(128)S(1)}, f32[128]{0:T(128)}, u32[]{:S(2)}) copy-start(f32[128]{0:T(128)} %param.11) | copy-start | bytes 1540
  19.8 4.4 %copy-start.1 = (f32[128]{0:T(128)S(1)}, f32[128]{0:T(128)}, u32[]{:S(2)}) copy-start(f32[128]{0:T(128)} %param.12) | copy-start | bytes 1540
  19.8 4.4 %copy-start.2 = (s32[2,128]{1,0:T(2,128)S(1)}, s32[2,128]{1,0:T(2,128)}, u32[]{:S(2)}) copy-start(s32[2,128]{1,0:T(2,128)} %doc_ref.1) | copy-start | bytes 3076
  19.9 4.3 %collective-permute-start.3 = (bf16[2,128,1024]{2,1,0:T(8,128)(2,1)S(1)}, bf16[2,128,1024]{2,1,0:T(8,128)(2,1)S(1)}, u32[]{:S(2)}, u32[]{:S(2)}) collective-permute-start(bf16[2,128,1024]{2,1,0:T(8,128)(2,1)S(1)} %broadcast_select_fusion), channel_id=1, source_target_pairs={{0,1},{1,0},{2,3},{3,2},{4,5},{5,4},{6,7},{7,6},{8,9},{9,8},{10,11... | collective-permute-start | bytes 1572872 | tf_op jit(solution)/shard_map/ppermute | solution.py:358
  37.3 14.0 %collective-permute-start.4 = (bf16[2,128,1024]{2,1,0:T(8,128)(2,1)}, bf16[2,128,1024]{2,1,0:T(8,128)(2,1)S(1)}, u32[]{:S(2)}, u32[]{:S(2)}) collective-permute-start(bf16[2,128,1024]{2,1,0:T(8,128)(2,1)} %get-tuple-element.45), channel_id=1, source_target_pairs={{0,1},{1,0},{2,3},{3,2},{4,5},{5,4},{6,7},{7,6},{8,9},{9,8},{10,11... | collective-permute-start | bytes 1572872 | tf_op jit(solution)/shard_map/ppermute | solution.py:358
  38.6 27.6 %all-to-all-start = ((f32[256,2,128]{2,1,0:T(2,128)}), f32[256,2,128]{2,1,0:T(2,128)S(1)}, u32[]{:S(2)}, u32[]{:S(2)}) async-start(f32[256,2,128]{2,1,0:T(2,128)} %broadcast_in_dim.55), calls=%async_computation | async-start | bytes 524288 | tf_op jit(solution)/shard_map/all_to_all | solution.py:428
  51.6 15.4 %collective-permute-start.5 = (bf16[2,128,1024]{2,1,0:T(8,128)(2,1)S(1)}, bf16[2,128,1024]{2,1,0:T(8,128)(2,1)S(1)}, u32[]{:S(2)}, u32[]{:S(2)}) collective-permute-start(bf16[2,128,1024]{2,1,0:T(8,128)(2,1)S(1)} %add_convert_fusion), channel_id=1, source_target_pairs={{1,2},{3,4},{5,6},{7,8},{9,10},{11,12},{13,14},{15,16},{17,18},{19... | collective-permute-start | bytes 1572872 | tf_op jit(solution)/shard_map/ppermute | solution.py:358
  55.0 17.0 %collective-permute-start.6 = (bf16[2,128,1024]{2,1,0:T(8,128)(2,1)S(1)}, bf16[2,128,1024]{2,1,0:T(8,128)(2,1)S(1)}, u32[]{:S(2)}, u32[]{:S(2)}) collective-permute-start(bf16[2,128,1024]{2,1,0:T(8,128)(2,1)S(1)} %get-tuple-element.47), channel_id=1, source_target_pairs={{2,0},{4,2},{6,4},{8,6},{10,8},{12,10},{14,12},{16,14},{18,16},{20... | collective-permute-start | bytes 1572872 | tf_op jit(solution)/shard_map/ppermute | solution.py:358
  58.1 13.8 %collective-permute-start.7 = (bf16[2,128,1024]{2,1,0:T(8,128)(2,1)S(1)}, bf16[2,128,1024]{2,1,0:T(8,128)(2,1)S(1)}, u32[]{:S(2)}, u32[]{:S(2)}) collective-permute-start(bf16[2,128,1024]{2,1,0:T(8,128)(2,1)S(1)} %get-tuple-element.48), channel_id=1, source_target_pairs={{0,1},{1,0},{2,3},{3,2},{4,5},{5,4},{6,7},{7,6},{8,9},{9,8},{10,11... | collective-permute-start | bytes 1572872 | tf_op jit(solution)/shard_map/ppermute | solution.py:358

commit v5 on v4

--- a/solution.py
+++ b/solution.py
@@ -30,6 +30,12 @@
 
 def half_turn(x):
     return pltpu.roll(x, x.shape[-1] // 2, 1)
+
+
+def lane_sums(blocks, terms):
+    size = blocks[0].shape[0]
+    total = lane_sum(jnp.concatenate(blocks, axis=0), terms)
+    return [total[i * size : (i + 1) * size] for i in range(len(blocks))]
 
 
 def lane_sum(x, terms):
@@ -42,9 +48,10 @@
     return contract(split, jnp.ones((terms * width, width), BF16), 1, 0)
 
 
-def normalize(x):
-    inverse = lax.rsqrt(lane_sum(x * x, 2) * (1.0 / x.shape[-1]) + norm_epsilon)
-    return x * inverse, inverse
+def normalize(blocks):
+    sums = lane_sums([x * x for x in blocks], 2)
+    inverses = [lax.rsqrt(s * (1.0 / s.shape[-1]) + norm_epsilon) for s in sums]
+    return [(x * inverse, inverse) for x, inverse in zip(blocks, inverses)]
 
 
 def rotate(raw, inverse, gain, cosine, sine):
@@ -54,10 +61,6 @@
 
 def unrotate(g, cosine, sine):
     return g * cosine + half_turn(g * sine)
-
-
-def norm_back(grad, normed, inverse):
-    return inverse * (grad - normed * (lane_sum(grad * normed, 1) * (1.0 / grad.shape[-1])))
 
 
 def contract(a, b, da, db):
@@ -76,8 +79,8 @@
         for r in range(q_ref.shape[2] // width):
             cols = slice(r * width, (r + 1) * width)
             jobs.append((x, q_ref, qr_ref, qi_ref, cols, gain_q_ref[...] * query_factor))
-    norms = [normalize(src[x, :, cols].astype(F32))[1] for x, src, _, _, cols, _ in jobs]
-    for inverse, (x, src, out, inv_out, cols, gain) in zip(norms, jobs):
+    norms = normalize([src[x, :, cols].astype(F32) for x, src, _, _, cols, _ in jobs])
+    for (_, inverse), (x, src, out, inv_out, cols, gain) in zip(norms, jobs):
         gain = jnp.broadcast_to(gain, inverse.shape)
         turned = rotate(src[x, :, cols], inverse, gain, cos_ref[x], sin_ref[x])
         out[x, :, cols] = turned.astype(BF16)
@@ -197,9 +200,10 @@
     cols = [slice(r * width, (r + 1) * width) for r in sides]
     raw_q = [[q_ref[x, :, cols[r]] for r in sides] for x in halves]
     raw_k = [(k_ref[x], near[0][x], far[0][x]) for x in halves]
+    arrived = normalize([raw_k[x][p].astype(F32) for x in halves for p in spans[1:]])
     k_norm = [
         [(raw_k[x][0].astype(F32) * ki_ref[x], ki_ref[x])]
-        + [normalize(raw_k[x][p].astype(F32)) for p in spans[1:]]
+        + arrived[x * (PANELS - 1) : (x + 1) * (PANELS - 1)]
         for x in halves
     ]
     q_rot = [jnp.concatenate([qr_ref[x, :, cols[r]] for r in sides], axis=0) for x in halves]
@@ -231,26 +235,39 @@
     attended = [contract(probs[x], vals[x], 0, 0) for x in halves]
     sum_q = jnp.zeros((1, width), F32)
     sum_k = jnp.zeros((1, width), F32)
+    work = []
     for x in halves:
         for p in spans:
             rows = slice(p * block, (p + 1) * block)
             normed, inverse = k_norm[x][p]
             back = unrotate(grad_k[x][rows], cos_ref[x, p], sin_ref[x, p])
             sum_k = sum_k + jnp.sum(back * normed, axis=0, keepdims=True)
-            raw = norm_back(back * gain_k, normed, inverse)
-            if p == 0:
-                own_k_ref[x] = raw
-                own_v_ref[x] = grad_v[x][rows]
-            else:
-                target = near_grad if p == 1 else far_grad
-                target.append((raw, grad_v[x][rows]))
+            work.append((back * gain_k, normed, inverse))
         for r in sides:
             rows = slice(r * block, (r + 1) * block)
             inverse = qi_ref[x, :, cols[r]]
             normed = raw_q[x][r].astype(F32) * inverse
             back = unrotate(grad_q[x][rows], cos_ref[x, 0], sin_ref[x, 0])
             sum_q = sum_q + jnp.sum(back * normed, axis=0, keepdims=True)
-            gq_ref[x, :, cols[r]] = norm_back(back * gain_q, normed, inverse).astype(BF16)
+            work.append((back * gain_q, normed, inverse))
+    means = lane_sums([grad * normed for grad, normed, _ in work], 1)
+    done = [
+        inverse * (grad - normed * (mean * (1.0 / width)))
+        for (grad, normed, inverse), mean in zip(work, means)
+    ]
+    for x in halves:
+        first = x * (PANELS + repeat)
+        for p in spans:
+            raw, value = done[first + p], grad_v[x][p * block : (p + 1) * block]
+            if p == 0:
+                own_k_ref[x] = raw
+                own_v_ref[x] = value
+            else:
+                target = near_grad if p == 1 else far_grad
+                target.append((raw, value))
+        for r in sides:
+            rows = slice(r * block, (r + 1) * block)
+            gq_ref[x, :, cols[r]] = done[first + PANELS + r].astype(BF16)
             att_ref[x, :, cols[r]] = attended[x][rows].astype(BF16)
     for part in range(2):
         low, high = near_grad[0][part], near_grad[1][part]

time: 74.9 us -> 75.8 us (1.012)
  Pallas kernels: 22.6 us -> 23.6 us
    pallas_call x1, Pallas kernels: 13.2 us -> 14.1 us  [attend(): pl.pallas_call(functools.partial(attend_kernel, group), grid=(heads,), in...]
  transfers between devices with their start and end apart: 9 -> 9, of which waited for: 3 -> 3; matrix products, arithmetic and copies ran while one was open for 7% -> 6% of each run, Pallas kernels for 9% -> 9%
where the time goes in v5:
time: 75.8 us; the launch traced here: 75.4 us
  starting transfers between devices  30.7 us (41%)
  Pallas kernels  23.6 us (31%)
  waiting for transfers between devices  13.2 us (17%)
  other arithmetic  4.48 us (6%)
  local copies, waits for them, and re-layouts  2.57 us (3%)
  between operations  0.81 us (1%)
    ppermute x8, starting transfers between devices, move(): return lax.ppermute(x, 'ctx', pairs)  18 us
    pallas_call x1, Pallas kernels, attend(): pl.pallas_call(functools.partial(attend_kernel, group), grid=(heads,), in...  14.1 us
    all_to_all x1, starting transfers between devices, shards(): lax.all_to_all(spread, ('dp', 'ctx'), 0, 0, tiled=True)  12.7 us
    all_to_all x1, waiting for transfers between devices, shards(): lax.all_to_all(spread, ('dp', 'ctx'), 0, 0, tiled=True)  7.18 us
    pallas_call x1, Pallas kernels, prepare(): pl.pallas_call(prepare_kernel, grid=(columns // width,), in_specs=[whole(...  6.99 us
    ppermute x8, waiting for transfers between devices, move(): return lax.ppermute(x, 'ctx', pairs)  6.01 us
    pallas_call x1, Pallas kernels, gather(): pl.pallas_call(gather_kernel, grid=(block // tile,), in_specs=[pl.BlockSp...  2.5 us
  transfers between devices with their start and end apart: 9, of which 3 were waited for; matrix products, arithmetic and copies ran while one was open for 6% of the time, Pallas kernels for 9%

profile of v5, /device:TPU:33, one launch (start us, length us, event | category | flops | bytes accessed | tf_op | source)
XLA Modules:
  0.0 75.4 jit_solution(14607212050218701225)
XLA Ops:
  0.6 1.3 %fusion.7 = (bf16[1,128,1024]{2,1,0:T(8,128)(2,1)S(1)}, bf16[1,128,1024]{2,1,0:T(8,128)(2,1)S(1)}, bf16[1,128,1024]{2,1,0:T(8,128)(2,1)S(1)}, bf16[1,128,1024]{2,1,0:T(8,128)(2,1)S(1)}) fusion(bf16[2,128,1024]{2,1,0:T(8,128)(2,1)} %k_ref.3, bf16[2,128,1024]{2,1,0:T(8,128)(2,1)} %v_ref.1), kind=kLoop, calls=%fused_computation.30 | loop fusion | bytes 2097152 | tf_op jit(solution)/shard_map/slice | solution.py:403
  1.9 0.9 %broadcast_select_fusion.1 = (bf16[2,128,1024]{2,1,0:T(8,128)(2,1)S(1)}, bf16[2,128,1024]{2,1,0:T(8,128)(2,1)}) fusion(pred[]{:T(512)S(6)} %eq.8, bf16[1,128,1024]{2,1,0:T(8,128)(2,1)S(1)} %get-tuple-element.71, bf16[1,128,1024]{2,1,0:T(8,128)(2,1)S(1)} %get-tuple-element.55, bf16[1,128,1024]{2,1,0:T(8,128)(2,1)S(1)} %get-tuple-element.72, ...), kind=kLoop, calls=%fused_computation.7 | loop fusion | flops 1048576 | bytes 2097153 | tf_op jit(solution)/shard_map/jit(_where)/select_n | solution.py:406
  2.8 4.2 %collective-permute-start.2 = (bf16[2,128,1024]{2,1,0:T(8,128)(2,1)}, bf16[2,128,1024]{2,1,0:T(8,128)(2,1)S(1)}, u32[]{:S(2)}, u32[]{:S(2)}) collective-permute-start(bf16[2,128,1024]{2,1,0:T(8,128)(2,1)} %get-tuple-element.53), channel_id=1, source_target_pairs={{0,2},{2,4},{4,6},{6,8},{8,10},{10,12},{12,14},{14,16},{16,18},{18... | collective-permute-start | bytes 1572872 | tf_op jit(solution)/shard_map/ppermute | solution.py:375
  7.0 0.1 collective-permute-start
  7.1 3.1 %collective-permute-start.1 = (bf16[2,128,1024]{2,1,0:T(8,128)(2,1)S(1)}, bf16[2,128,1024]{2,1,0:T(8,128)(2,1)S(1)}, u32[]{:S(2)}, u32[]{:S(2)}) collective-permute-start(bf16[2,128,1024]{2,1,0:T(8,128)(2,1)S(1)} %get-tuple-element.52), channel_id=1, source_target_pairs={{1,2},{3,4},{5,6},{7,8},{9,10},{11,12},{13,14},{15,16},{17,18},{19... | collective-permute-start | bytes 1572872 | tf_op jit(solution)/shard_map/ppermute | solution.py:375
  10.2 0.1 pad_add_fusion
  10.2 0.1 compare_and_fusion
  10.3 0.1 fusion.6
  10.4 0.1 select_convert_fusion
  10.5 1.5 %fusion.4 = (f32[2,3,128,64]{3,2,1,0:T(8,128)S(1)}, f32[2,3,128,64]{3,2,1,0:T(8,128)S(1)}, f32[2,3,128,64]{3,2,1,0:T(8,128)S(1)}) fusion(f32[64]{0:T(128)S(1)} %multiply_exponential_fusion, f32[2,3,128]{2,1,0:T(4,128)S(1)} %select_convert_fusion), kind=kLoop, calls=%fused_computation.19 | loop fusion | flops 98304 | bytes 593152 | tf_op jit(solution)/shard_map/neg | solution.py:417
  11.9 0.8 %fusion.1 = (f32[2,128,128]{2,1,0:T(8,128)}, f32[2,128,128]{2,1,0:T(8,128)}) fusion(f32[2,3,128,64]{3,2,1,0:T(8,128)S(1)} %get-tuple-element.58, f32[2,3,128,64]{3,2,1,0:T(8,128)S(1)} %get-tuple-element.59, f32[2,3,128,64]{3,2,1,0:T(8,128)S(1)} %get-tuple-element.60), kind=kLoop, calls=%fused_computation.16 | loop fusion | flops 65536 | bytes 851968 | tf_op jit(solution)/shard_map/squeeze | solution.py:418
  12.8 7.0 %prepare.1 = (bf16[2,128,2048]{2,1,0:T(8,128)(2,1)}, f32[2,128,2048]{2,1,0:T(8,128)}, bf16[2,128,1024]{2,1,0:T(8,128)(2,1)}, f32[2,128,1024]{2,1,0:T(8,128)}) custom-call(f32[1,128]{1,0:T(1,128)} %bitcast.12, f32[1,128]{1,0:T(1,128)} %bitcast.14, f32[2,128,128]{2,1,0:T(8,128)} %get-tuple-element.70.cos_ref, f32[2,128,128]{2,1,0:T(8,128)} %get-tuple-element.69.sin_ref, ...), custom_call_target="tpu_custom_call" | custom-call | flops 33554432 | bytes 8388608 | tf_op jit(solution)/shard_map/prepare/pallas_call | solution.py:97
  19.8 0.0 copy-start
  19.8 0.0 copy-start.1
  19.8 0.1 broadcast_select_fusion
  19.9 2.7 %collective-permute-start.3 = (bf16[2,128,1024]{2,1,0:T(8,128)(2,1)S(1)}, bf16[2,128,1024]{2,1,0:T(8,128)(2,1)S(1)}, u32[]{:S(2)}, u32[]{:S(2)}) collective-permute-start(bf16[2,128,1024]{2,1,0:T(8,128)(2,1)S(1)} %broadcast_select_fusion), channel_id=1, source_target_pairs={{0,1},{1,0},{2,3},{3,2},{4,5},{5,4},{6,7},{7,6},{8,9},{9,8},{10,11... | collective-permute-start | bytes 1572872 | tf_op jit(solution)/shard_map/ppermute | solution.py:375
  22.6 0.3 pad_maximum_fusion.2
  22.9 1.2 %collective-permute-done.3.relay_ref = bf16[2,128,1024]{2,1,0:T(8,128)(2,1)S(1)} collective-permute-done((bf16[2,128,1024]{2,1,0:T(8,128)(2,1)S(1)}, bf16[2,128,1024]{2,1,0:T(8,128)(2,1)S(1)}, u32[]{:S(2)}, u32[]{:S(2)}) %collective-permute-start.3) | collective-permute-done | bytes 524320 | tf_op jit(solution)/shard_map/ppermute | solution.py:375
  24.2 14.1 %attend.1 = (bf16[2,128,2048]{2,1,0:T(8,128)(2,1)}, bf16[2,128,2048]{2,1,0:T(8,128)(2,1)}, f32[2,128,1024]{2,1,0:T(8,128)}, f32[2,128,1024]{2,1,0:T(8,128)}, bf1...) custom-call(s32[1]{0:T(128)} %bitcast.index_ref, ...), custom_call_target="tpu_custom_call" | custom-call | flops 2415919104 | bytes 12582912 | tf_op jit(solution)/shard_map/attend/pallas_call | solution.py:294
  38.3 0.5 collective-permute-start.4
  38.8 0.8 %broadcast_in_dim.55 = f32[256,2,128]{2,1,0:T(2,128)} broadcast(f32[2,128]{1,0:T(2,128)S(1)} %get-tuple-element.51), dimensions={1,2} | broadcast | bytes 263168 | tf_op jit(solution)/shard_map/broadcast_in_dim | solution.py:444
  39.5 12.7 %all-to-all-start = ((f32[256,2,128]{2,1,0:T(2,128)}), f32[256,2,128]{2,1,0:T(2,128)S(1)}, u32[]{:S(2)}, u32[]{:S(2)}) async-start(f32[256,2,128]{2,1,0:T(2,128)} %broadcast_in_dim.55), calls=%async_computation | async-start | bytes 524288 | tf_op jit(solution)/shard_map/all_to_all | solution.py:445
  52.3 0.2 add_convert_fusion
  52.5 3.4 %collective-permute-start.5 = (bf16[2,128,1024]{2,1,0:T(8,128)(2,1)S(1)}, bf16[2,128,1024]{2,1,0:T(8,128)(2,1)S(1)}, u32[]{:S(2)}, u32[]{:S(2)}) collective-permute-start(bf16[2,128,1024]{2,1,0:T(8,128)(2,1)S(1)} %add_convert_fusion), channel_id=1, source_target_pairs={{1,2},{3,4},{5,6},{7,8},{9,10},{11,12},{13,14},{15,16},{17,18},{19... | collective-permute-start | bytes 1572872 | tf_op jit(solution)/shard_map/ppermute | solution.py:375
  55.9 3.2 %collective-permute-start.6 = (bf16[2,128,1024]{2,1,0:T(8,128)(2,1)S(1)}, bf16[2,128,1024]{2,1,0:T(8,128)(2,1)S(1)}, u32[]{:S(2)}, u32[]{:S(2)}) collective-permute-start(bf16[2,128,1024]{2,1,0:T(8,128)(2,1)S(1)} %get-tuple-element.47), channel_id=1, source_target_pairs={{2,0},{4,2},{6,4},{8,6},{10,8},{12,10},{14,12},{16,14},{18,16},{20... | collective-permute-start | bytes 1572872 | tf_op jit(solution)/shard_map/ppermute | solution.py:375
  59.1 0.9 %collective-permute-start.7 = (bf16[2,128,1024]{2,1,0:T(8,128)(2,1)S(1)}, bf16[2,128,1024]{2,1,0:T(8,128)(2,1)S(1)}, u32[]{:S(2)}, u32[]{:S(2)}) collective-permute-start(bf16[2,128,1024]{2,1,0:T(8,128)(2,1)S(1)} %get-tuple-element.48), channel_id=1, source_target_pairs={{0,1},{1,0},{2,3},{3,2},{4,5},{5,4},{6,7},{7,6},{8,9},{9,8},{10,11... | collective-permute-start | bytes 1572872 | tf_op jit(solution)/shard_map/ppermute | solution.py:375
  60.0 7.2 %all-to-all-done = f32[256,2,128]{2,1,0:T(2,128)S(1)} async-done(((f32[256,2,128]{2,1,0:T(2,128)}), f32[256,2,128]{2,1,0:T(2,128)S(1)}, u32[]{:S(2)}, u32[]{:S(2)}) %all-to-all-start) | async-done | bytes 262176 | tf_op jit(solution)/shard_map/all_to_all | solution.py:445
  67.1 0.3 reduce_sum.9
  67.4 0.5 slice_bitcast_fusion
  67.9 0.2 select_add_fusion.cross_ref
  68.1 4.7 %collective-permute-done.6.skip_ref = bf16[2,128,1024]{2,1,0:T(8,128)(2,1)S(1)} collective-permute-done((bf16[2,128,1024]{2,1,0:T(8,128)(2,1)S(1)}, bf16[2,128,1024]{2,1,0:T(8,128)(2,1)S(1)}, u32[]{:S(2)}, u32[]{:S(2)}) %collective-permute-start.6) | collective-permute-done | bytes 524320 | tf_op jit(solution)/shard_map/ppermute | solution.py:375
  72.9 2.5 %gather.1 = (bf16[2,128,1024]{2,1,0:T(8,128)(2,1)}, bf16[2,128,1024]{2,1,0:T(8,128)(2,1)}) custom-call(s32[1]{0:T(128)} %bitcast.index_ref, f32[2,128,1024]{2,1,0:T(8,128)} %get-tuple-element.40.own_k_ref, f32[2,128,1024]{2,1,0:T(8,128)} %get-tuple-element.41.own_v_ref, f32[2,128,1024]{2,1,0:T(8,128)S(1)} %select_add_fusion.cross_ref, ...), custom_call_target="tpu_custom_call" | custom-call | flops 2097152 | bytes 4194304 | tf_op jit(solution)/shard_map/gather/pallas_call | solution.py:356
  (11 shorter events, 0.0 us)
Async XLA Ops:
  2.8 20.1 %collective-permute-start.2 = (bf16[2,128,1024]{2,1,0:T(8,128)(2,1)}, bf16[2,128,1024]{2,1,0:T(8,128)(2,1)S(1)}, u32[]{:S(2)}, u32[]{:S(2)}) collective-permute-start(bf16[2,128,1024]{2,1,0:T(8,128)(2,1)} %get-tuple-element.53), channel_id=1, source_target_pairs={{0,2},{2,4},{4,6},{6,8},{8,10},{10,12},{12,14},{14,16},{16,18},{18... | collective-permute-start | bytes 1572872 | tf_op jit(solution)/shard_map/ppermute | solution.py:375
  7.0 15.9 %collective-permute-start = (bf16[2,128,1024]{2,1,0:T(8,128)(2,1)}, bf16[2,128,1024]{2,1,0:T(8,128)(2,1)S(1)}, u32[]{:S(2)}, u32[]{:S(2)}) collective-permute-start(bf16[2,128,1024]{2,1,0:T(8,128)(2,1)} %get-tuple-element.53), channel_id=1, source_target_pairs={{0,1},{1,0},{2,3},{3,2},{4,5},{5,4},{6,7},{7,6},{8,9},{9,8},{10,11... | collective-permute-start | bytes 1572872 | tf_op jit(solution)/shard_map/ppermute | solution.py:375
  7.1 12.7 %collective-permute-start.1 = (bf16[2,128,1024]{2,1,0:T(8,128)(2,1)S(1)}, bf16[2,128,1024]{2,1,0:T(8,128)(2,1)S(1)}, u32[]{:S(2)}, u32[]{:S(2)}) collective-permute-start(bf16[2,128,1024]{2,1,0:T(8,128)(2,1)S(1)} %get-tuple-element.52), channel_id=1, source_target_pairs={{1,2},{3,4},{5,6},{7,8},{9,10},{11,12},{13,14},{15,16},{17,18},{19... | collective-permute-start | bytes 1572872 | tf_op jit(solution)/shard_map/ppermute | solution.py:375
  19.8 4.4 %copy-start = (f32[128]{0:T(128)S(1)}, f32[128]{0:T(128)}, u32[]{:S(2)}) copy-start(f32[128]{0:T(128)} %param.11) | copy-start | bytes 1540
  19.8 4.4 %copy-start.1 = (f32[128]{0:T(128)S(1)}, f32[128]{0:T(128)}, u32[]{:S(2)}) copy-start(f32[128]{0:T(128)} %param.12) | copy-start | bytes 1540
  19.8 4.4 %copy-start.2 = (s32[2,128]{1,0:T(2,128)S(1)}, s32[2,128]{1,0:T(2,128)}, u32[]{:S(2)}) copy-start(s32[2,128]{1,0:T(2,128)} %doc_ref.1) | copy-start | bytes 3076
  19.9 4.3 %collective-permute-start.3 = (bf16[2,128,1024]{2,1,0:T(8,128)(2,1)S(1)}, bf16[2,128,1024]{2,1,0:T(8,128)(2,1)S(1)}, u32[]{:S(2)}, u32[]{:S(2)}) collective-permute-start(bf16[2,128,1024]{2,1,0:T(8,128)(2,1)S(1)} %broadcast_select_fusion), channel_id=1, source_target_pairs={{0,1},{1,0},{2,3},{3,2},{4,5},{5,4},{6,7},{7,6},{8,9},{9,8},{10,11... | collective-permute-start | bytes 1572872 | tf_op jit(solution)/shard_map/ppermute | solution.py:375
  38.3 14.0 %collective-permute-start.4 = (bf16[2,128,1024]{2,1,0:T(8,128)(2,1)}, bf16[2,128,1024]{2,1,0:T(8,128)(2,1)S(1)}, u32[]{:S(2)}, u32[]{:S(2)}) collective-permute-start(bf16[2,128,1024]{2,1,0:T(8,128)(2,1)} %get-tuple-element.45), channel_id=1, source_target_pairs={{0,1},{1,0},{2,3},{3,2},{4,5},{5,4},{6,7},{7,6},{8,9},{9,8},{10,11... | collective-permute-start | bytes 1572872 | tf_op jit(solution)/shard_map/ppermute | solution.py:375
  39.5 27.6 %all-to-all-start = ((f32[256,2,128]{2,1,0:T(2,128)}), f32[256,2,128]{2,1,0:T(2,128)S(1)}, u32[]{:S(2)}, u32[]{:S(2)}) async-start(f32[256,2,128]{2,1,0:T(2,128)} %broadcast_in_dim.55), calls=%async_computation | async-start | bytes 524288 | tf_op jit(solution)/shard_map/all_to_all | solution.py:445
  52.5 15.4 %collective-permute-start.5 = (bf16[2,128,1024]{2,1,0:T(8,128)(2,1)S(1)}, bf16[2,128,1024]{2,1,0:T(8,128)(2,1)S(1)}, u32[]{:S(2)}, u32[]{:S(2)}) collective-permute-start(bf16[2,128,1024]{2,1,0:T(8,128)(2,1)S(1)} %add_convert_fusion), channel_id=1, source_target_pairs={{1,2},{3,4},{5,6},{7,8},{9,10},{11,12},{13,14},{15,16},{17,18},{19... | collective-permute-start | bytes 1572872 | tf_op jit(solution)/shard_map/ppermute | solution.py:375
  55.9 17.0 %collective-permute-start.6 = (bf16[2,128,1024]{2,1,0:T(8,128)(2,1)S(1)}, bf16[2,128,1024]{2,1,0:T(8,128)(2,1)S(1)}, u32[]{:S(2)}, u32[]{:S(2)}) collective-permute-start(bf16[2,128,1024]{2,1,0:T(8,128)(2,1)S(1)} %get-tuple-element.47), channel_id=1, source_target_pairs={{2,0},{4,2},{6,4},{8,6},{10,8},{12,10},{14,12},{16,14},{18,16},{20... | collective-permute-start | bytes 1572872 | tf_op jit(solution)/shard_map/ppermute | solution.py:375
  59.1 13.8 %collective-permute-start.7 = (bf16[2,128,1024]{2,1,0:T(8,128)(2,1)S(1)}, bf16[2,128,1024]{2,1,0:T(8,128)(2,1)S(1)}, u32[]{:S(2)}, u32[]{:S(2)}) collective-permute-start(bf16[2,128,1024]{2,1,0:T(8,128)(2,1)S(1)} %get-tuple-element.48), channel_id=1, source_target_pairs={{0,1},{1,0},{2,3},{3,2},{4,5},{5,4},{6,7},{7,6},{8,9},{9,8},{10,11... | collective-permute-start | bytes 1572872 | tf_op jit(solution)/shard_map/ppermute | solution.py:375
